TPU v7x, 128 devices: a whole 4x4x4 slice. The times are simulated.
128 devices in a mesh: gx: 8 (over y, core), gy: 16 (over x, z).
Axes of the slice: x: 4, y: 4, z: 4, core: 2. Of those that a mesh axis runs over, the one named last changes fastest.
Arguments:
- owned_surplus: float32 [16384, 16, 256], P(('gx', 'gy')), may hold values from -0.6 to 0.6
- tile_owner: int32 [16384], replicated, may hold values from 0 to 127, as said below
- grid_levels: int32 [8, 2], replicated, may hold values from 0 to 3, as said below
- coefficients: int32 [8], replicated, may hold values from 1 to 3
- faulty_grids: int32 [2], replicated, may hold values from 1 to 7
- velocity_x: float32 [4096, 16384], P('gx', 'gy'), may hold values from -1 to 1
- velocity_y: float32 [4096, 16384], P('gx', 'gy'), may hold values from -1 to 1
Outputs:
- solution: float32 [4096, 16384], P('gx', 'gy')
Inputs may be any that keep to these rules, and one draw needn't show every extreme that they name: tile_owner[d * 128 + k] = (d + o_k) mod (the number of devices), with offsets o_k that depend only on k; no offset value serves more than 2 of the 128 values of k, and some offset value serves exactly 2. `grid_levels`: row 0 is (0, 0), the full grid.
All inputs are finite; a program needn't handle non-finite values.
Results may differ from a plain program's by a relative error of at most 0.00011.
Values sent between devices are 32-bit elements; how exact they have to be, the bound alone decides.
No kernel may reach another device: no remote copies, remote signals or barrier semaphores. Data moves between devices by JAX's collectives and lax.ppermute only.
A program may use at most 128 MiB of HBM per device.

v0:
```python
import functools

import jax
import jax.numpy as jnp
from jax import lax
from jax.experimental import pallas as pl
from jax.experimental.pallas import tpu as pltpu
from jax.sharding import PartitionSpec as P

STEPS = 2
TIME_STEP = 0.2
DIFFUSION = 0.5
HALO = 8
LANES = 128
HAT = 256
VMEM_LIMIT = 48 << 20


def pack_kernel(tiles_across, capacity, target_ref, rank_ref, owned_ref, outgoing_ref):
    count, tile_rows, _ = owned_ref.shape
    messages = outgoing_ref.shape[0]
    half = tile_rows
    rows = []
    for ky in range(tiles_across):
        rows += [owned_ref[ky, 0:1, :LANES], owned_ref[ky, 0:1, LANES:]]
    per_part = LANES // tile_rows
    for part in range(count // tiles_across // per_part):
        columns = [
            owned_ref[(part * per_part + t) * tiles_across, :, :LANES] for t in range(per_part)
        ]
        rows.append(jnp.concatenate(columns, axis=0).T[0:1])
    rows += [rows[0]] * 4
    lead = jnp.concatenate(rows, axis=0)

    def address(m, carry):
        outgoing_ref[m, pl.ds(2 * half * capacity, lead.shape[0]), :] = lead
        return carry

    lax.fori_loop(0, messages, address, 0, unroll=8)

    def place(k, carry):
        m = target_ref[k]
        row = pl.multiple_of(rank_ref[k] * (2 * half), 2 * half)
        outgoing_ref[m, pl.ds(row, half), :] = owned_ref[k, :, :LANES]
        outgoing_ref[m, pl.ds(row + half, half), :] = owned_ref[k, :, LANES:]
        return carry

    lax.fori_loop(0, count, place, 0, unroll=8)


def pack(target, rank, owned, messages, capacity, tiles_across):
    count, tile_rows, _ = owned.shape
    lead_rows = 2 * tiles_across + count // tiles_across * tile_rows // LANES + 4
    smem = pl.BlockSpec(memory_space=pltpu.SMEM)
    vmem = pl.BlockSpec(memory_space=pltpu.VMEM)
    return pl.pallas_call(
        functools.partial(pack_kernel, tiles_across, capacity),
        out_shape=jax.ShapeDtypeStruct(
            (messages, capacity * tile_rows * 2 + lead_rows, LANES), owned.dtype
        ),
        in_specs=[smem, smem, vmem],
        out_specs=vmem,
        compiler_params=pltpu.CompilerParams(vmem_limit_bytes=VMEM_LIMIT),
        name="pack_tiles",
    )(target, rank, owned)


def split_dot(left, right, split_left):
    value = left if split_left else right
    high = value.astype(jnp.bfloat16)
    low = (value - high.astype(jnp.float32)).astype(jnp.bfloat16)
    if split_left:
        pairs = ((high, right), (low, right))
    else:
        pairs = ((left, high), (left, low))
    return sum(jnp.dot(a, b, preferred_element_type=jnp.float32) for a, b in pairs)


def refine_kernel(
    tiles_across, tile_rows, capacity, source_ref, rank_ref, incoming_ref, share_ref, weight_ref,
    hat_x_ref, hat_y_ref, nodal_ref, first_rows_ref, last_rows_ref, left_ref, right_ref,
    block, edge,
):
    height = nodal_ref.shape[1]
    tiles_down = height // tile_rows
    row_parts = 2 * tiles_across
    col_parts = height // LANES
    lead_row = 2 * tile_rows * capacity
    lead_size = share_ref.shape[2]
    tile_weight = jnp.concatenate([weight_ref[...]] * (tile_rows // 8), axis=0)

    def place(kx, carry):
        row = pl.multiple_of(kx * tile_rows, tile_rows)
        for ky in range(tiles_across):
            message = source_ref[kx * tiles_across + ky]
            start = pl.multiple_of(rank_ref[kx * tiles_across + ky] * (2 * tile_rows), 2 * tile_rows)
            for part in range(2):
                block[pl.ds(row, tile_rows), (2 * ky + part) * LANES : (2 * ky + part + 1) * LANES] = (
                    incoming_ref[message, pl.ds(start + part * tile_rows, tile_rows), :] * tile_weight
                )
        return carry

    lax.fori_loop(0, tiles_down, place, 0, unroll=2)

    def collect(m, sums):
        lead = incoming_ref[m, pl.ds(lead_row, lead_size), :]
        return tuple(total + share_ref[i, m] * lead for i, total in enumerate(sums))

    zero = jnp.zeros((lead_size, LANES), jnp.float32)
    own_lead, next_lead = lax.fori_loop(0, incoming_ref.shape[0], collect, (zero, zero), unroll=8)

    weight = weight_ref[...]
    lane = lax.broadcasted_iota(jnp.int32, (1, LANES), 1)
    corner_base = row_parts + col_parts
    corner = lambda x: weight[0:1, 0:1] * jnp.where(
        lane == 0,
        own_lead[corner_base + 2 * x : corner_base + 2 * x + 1, 0:1],
        own_lead[corner_base + 2 * x + 1 : corner_base + 2 * x + 2, 0:1],
    )
    for part in range(col_parts):
        pair = jnp.concatenate(
            [
                own_lead[row_parts + part : row_parts + part + 1],
                next_lead[row_parts + part : row_parts + part + 1],
                jnp.zeros((LANES - 2, LANES), jnp.float32),
            ],
            axis=0,
        ).T
        edge[part * LANES : (part + 1) * LANES, :] = (
            pair.reshape(LANES // 8, 8, LANES) * weight[:, 0:1][None]
        ).reshape(LANES, LANES)

    row_id = lax.broadcasted_iota(jnp.int32, (HAT, HAT), 0)
    lane_id = lax.broadcasted_iota(jnp.int32, (HAT, HAT), 1)
    ramp_rows = row_id.astype(jnp.float32) * (1.0 / HAT)
    ramp_lanes = lane_id.astype(jnp.float32) * (1.0 / HAT)

    def refine_down(target, lanes, own, after):
        width = own.shape[1]
        middle = target[HAT : HAT + 1, lanes] + 0.5 * (own + after)
        for part, (first, last) in enumerate(((own, middle), (middle, after))):
            rows = slice(part * HAT, (part + 1) * HAT)
            values = jnp.where(row_id[:, :width] == 0, first, target[rows, lanes])
            target[rows, lanes] = split_dot(hat_x_ref[...], values, False) + ramp_rows[:, :width] * last

    refine_down(edge, slice(0, LANES), corner(0), corner(1))
    line = lambda lead, ky: (
        jnp.concatenate([lead[2 * ky : 2 * ky + 1], lead[2 * ky + 1 : 2 * ky + 2]], axis=1)
        * jnp.concatenate([weight[0:1]] * 2, axis=1)
    )
    for ky in range(tiles_across):
        refine_down(
            block, slice(ky * HAT, (ky + 1) * HAT), line(own_lead, ky), line(next_lead, ky)
        )
    for part in range(height // HAT):
        rows = slice(part * HAT, (part + 1) * HAT)
        ends = [edge[rows, 0:1], None, None, None, edge[rows, 1:2]]
        for middle, before, after in ((2, 0, 4), (1, 0, 2), (3, 2, 4)):
            ends[middle] = block[rows, middle * HAT : middle * HAT + 1] + 0.5 * (
                ends[before] + ends[after]
            )
        for ky in range(tiles_across):
            values = jnp.where(lane_id == 0, ends[ky], block[rows, ky * HAT : (ky + 1) * HAT])
            result = split_dot(values, hat_y_ref[...], True) + ramp_lanes * ends[ky + 1]
            nodal_ref[2 * ky, rows, :] = result[:, :LANES]
            nodal_ref[2 * ky + 1, rows, :] = result[:, LANES:]
            columns = slice(ky * HAT, (ky + 1) * HAT)
            if part == 0:
                first_rows_ref[:, columns] = result[:HALO]
            if part == height // HAT - 1:
                last_rows_ref[:, columns] = result[-HALO:]
            if ky == 0:
                left_ref[:, rows] = result[:, :LANES].T[:HALO]
            if ky == tiles_across - 1:
                right_ref[:, rows] = result[:, LANES:].T[-HALO:]


def refine_block(source, rank, incoming, share, weight, hat_x, hat_y, height, width, tile_rows, capacity):
    vmem = pl.BlockSpec(memory_space=pltpu.VMEM)
    smem = pl.BlockSpec(memory_space=pltpu.SMEM)
    shapes = [(width // LANES, height, LANES)] + [(HALO, width)] * 2 + [(HALO, height)] * 2
    return pl.pallas_call(
        functools.partial(refine_kernel, width // HAT, tile_rows, capacity),
        out_shape=[jax.ShapeDtypeStruct(shape, jnp.float32) for shape in shapes],
        in_specs=[smem, smem] + [vmem] * 5,
        out_specs=[vmem] * len(shapes),
        scratch_shapes=[
            pltpu.VMEM((height, width), jnp.float32), pltpu.VMEM((height, LANES), jnp.float32)
        ],
        compiler_params=pltpu.CompilerParams(vmem_limit_bytes=VMEM_LIMIT),
        name="refine_block",
    )(source, rank, incoming, share, weight, hat_x, hat_y)


def fill_halo(target, height, width, above, below, left, right, above_side, below_side):
    tiles = width // LANES
    first = 2 * HALO
    end = first + height
    for t in range(tiles):
        target[t, HALO:first, :] = above[:, t * LANES : (t + 1) * LANES]
        target[t, end : end + HALO, :] = below[:, t * LANES : (t + 1) * LANES]
    between = jnp.zeros((LANES - 2 * HALO, height), jnp.float32)
    target[tiles, first:end, :] = jnp.concatenate([right, between, left], axis=0).T
    target[tiles, HALO:first, :] = above_side
    target[tiles, end : end + HALO, :] = below_side


def edges_kernel(*refs):
    first_rows, last_rows, first_cols, last_cols = refs[8:]
    for f in range(2):
        top, bottom, left, right = refs[4 * f : 4 * f + 4]
        first_rows[f] = top[...]
        last_rows[f] = bottom[...]
        first_cols[f] = left[...].T[:HALO]
        last_cols[f] = right[...].T[-HALO:]


def edges(x, y):
    height, width = x.shape
    specs = [
        pl.BlockSpec((HALO, width), lambda i: (0, 0)),
        pl.BlockSpec((HALO, width), lambda i: (height // HALO - 1, 0)),
        pl.BlockSpec((height, LANES), lambda i: (0, 0)),
        pl.BlockSpec((height, LANES), lambda i: (0, width // LANES - 1)),
    ]
    shapes = [(2, HALO, width)] * 2 + [(2, HALO, height)] * 2
    return pl.pallas_call(
        edges_kernel,
        grid=(1,),
        out_shape=[jax.ShapeDtypeStruct(shape, jnp.float32) for shape in shapes],
        in_specs=specs * 2,
        out_specs=[pl.BlockSpec(shape, lambda i: (0, 0, 0)) for shape in shapes],
        name="velocity_edges",
    )(*[x] * 4, *[y] * 4)


def steps_kernel(
    chunk, last_chunk, nodal_ref, x_ref, y_ref, stencil_ref, rows_above, rows_below, speed_above,
    speed_below, speed_left, speed_right, from_left, from_right, out_ref, field, middle, speed,
):
    tiles, height, _ = nodal_ref.shape
    width = tiles * LANES
    count = tiles + 1
    scale = TIME_STEP * DIFFUSION / 12.0
    speed_scale = TIME_STEP / 12.0
    side = lax.broadcasted_iota(jnp.int32, (HALO, LANES), 1)

    def corner(k):
        part = slice(height + k * LANES, height + (k + 1) * LANES)
        return jnp.where(side < LANES // 2, from_right[:, part], from_left[:, part])

    for t in range(tiles):
        field[t, 2 * HALO : 2 * HALO + height, :] = nodal_ref[t]
    fill_halo(
        field, height, width, rows_above, rows_below, from_left[:, :height], from_right[:, :height],
        corner(0), corner(1),
    )
    for f, velocity in enumerate((x_ref, y_ref)):
        for t in range(tiles):
            speed[f, t, 2 * HALO : 2 * HALO + height, :] = (
                velocity[:, t * LANES : (t + 1) * LANES] * speed_scale
            )
        fill_halo(
            speed.at[f], height, width, speed_above[f] * speed_scale, speed_below[f] * speed_scale,
            speed_left[f] * speed_scale, speed_right[f] * speed_scale,
            corner(2 + 2 * f) * speed_scale, corner(3 + 2 * f) * speed_scale,
        )

    def advance(source, start, size, tile_range, store):
        parts = {}
        lane = lax.broadcasted_iota(jnp.int32, (size, LANES), 1)

        def split(t):
            if t not in parts:
                value = source[t, pl.ds(start, size), :]
                high = value.astype(jnp.bfloat16)
                parts[t] = (high, (value - high.astype(jnp.float32)).astype(jnp.bfloat16))
            return parts[t]

        for t in tile_range:
            before, after = split((t - 1) % count), split((t + 1) % count)
            around = [jnp.where(lane >= LANES // 2, b, a) for b, a in zip(before, after)]
            across = jnp.dot(
                jnp.concatenate([*split(t), *around], axis=1),
                stencil_ref[...],
                preferred_element_type=jnp.float32,
            )
            here = source[t, pl.ds(start, size), :]
            one_below = source[t, pl.ds(start - 1, size), :]
            one_above = source[t, pl.ds(start + 1, size), :]
            two_below = source[t, pl.ds(start - 2, size), :]
            two_above = source[t, pl.ds(start + 2, size), :]
            curve = 16.0 * (one_above + one_below) - (two_above + two_below) + across[:, :LANES]
            slope = 8.0 * (one_above - one_below) - (two_above - two_below)
            change = scale * curve - speed[0, t, pl.ds(start, size), :] * slope
            change = change - speed[1, t, pl.ds(start, size), :] * across[:, LANES:]
            store(t, (1.0 - 60.0 * scale) * here + change)

    def first_half(c, carry):
        start = pl.multiple_of(HALO + c * chunk, HALO)

        def store(t, result):
            middle[t, pl.ds(start, chunk), :] = result

        advance(field, start, chunk, range(count), store)
        return carry

    def second_half(c, carry):
        start = pl.multiple_of(HALO + c * chunk, HALO)

        def store(t, result):
            field[t, pl.ds(start, chunk), :] = 0.5 * (field[t, pl.ds(start, chunk), :] + result)

        advance(middle, start, chunk, range(count), store)
        return carry

    def last_half(c, carry):
        start = pl.multiple_of(2 * HALO + c * last_chunk, HALO)
        place = pl.multiple_of(c * last_chunk, HALO)

        def store(t, result):
            out_ref[pl.ds(place, last_chunk), t * LANES : (t + 1) * LANES] = 0.5 * (
                field[t, pl.ds(start, last_chunk), :] + result
            )

        advance(middle, start, last_chunk, range(tiles), store)
        return carry

    extended = (height + 2 * HALO) // chunk
    for step in range(STEPS):
        lax.fori_loop(0, extended, first_half, 0)
        if step < STEPS - 1:
            lax.fori_loop(0, extended, second_half, 0)
    lax.fori_loop(0, height // last_chunk, last_half, 0)


def largest_chunk(rows, limit):
    return max(size for size in range(16, limit + 1, 16) if rows % size == 0)


def run_steps(nodal, x, y, stencil, *halo):
    tiles, height, _ = nodal.shape
    vmem = pl.BlockSpec(memory_space=pltpu.VMEM)
    extended = (tiles + 1, height + 4 * HALO, LANES)
    return pl.pallas_call(
        functools.partial(
            steps_kernel, largest_chunk(height + 2 * HALO, 192), largest_chunk(height, 192)
        ),
        out_shape=jax.ShapeDtypeStruct((height, tiles * LANES), jnp.float32),
        in_specs=[vmem] * (4 + len(halo)),
        out_specs=vmem,
        scratch_shapes=[
            pltpu.VMEM(extended, jnp.float32),
            pltpu.VMEM(extended, jnp.float32),
            pltpu.VMEM((2,) + extended, jnp.float32),
        ],
        compiler_params=pltpu.CompilerParams(vmem_limit_bytes=VMEM_LIMIT),
        name="heun_steps",
    )(nodal, x, y, stencil, *halo)


def stencil_matrix():
    row = lax.broadcasted_iota(jnp.int32, (4 * LANES, 2 * LANES), 0)
    column = lax.broadcasted_iota(jnp.int32, (4 * LANES, 2 * LANES), 1)
    lane = row % LANES
    outside = jnp.where(lane < LANES // 2, lane + LANES, lane - LANES)
    shift = jnp.where(row < 2 * LANES, lane, outside) - column % LANES
    distance = jnp.abs(shift)
    curve = jnp.where(distance == 1, 16.0, jnp.where(distance == 2, -1.0, 0.0))
    slope = jnp.where(distance == 1, 8.0, jnp.where(distance == 2, -1.0, 0.0)) * jnp.sign(
        shift
    ).astype(jnp.float32)
    return jnp.where(column < LANES, curve, slope).astype(jnp.bfloat16)


def hat_matrix(size):
    place = lax.broadcasted_iota(jnp.int32, (size, size), 0)
    node = lax.broadcasted_iota(jnp.int32, (size, size), 1)
    return jnp.where(node == 0, 1.0 - place.astype(jnp.float32) / size, hat_value(node, place))


def hat_value(node, place):
    spacing = jnp.maximum(node & (-node), 1).astype(jnp.float32)
    return jnp.maximum(0.0, 1.0 - jnp.abs(place - node).astype(jnp.float32) / spacing)


def coarse_share(node, place):
    return jnp.where(node == 0, 1.0, hat_value(node, place))


def weight_pattern(grid_levels, coefficients, faulty_grids):
    grid_ids = jnp.arange(coefficients.shape[0], dtype=jnp.int32)
    alive = jnp.all(faulty_grids[None, :] != grid_ids[:, None], axis=1)
    share = jnp.where(alive, coefficients, 0).astype(jnp.float32)
    row = lax.broadcasted_iota(jnp.int32, (8, LANES), 0)[None]
    lane = lax.broadcasted_iota(jnp.int32, (8, LANES), 1)[None]
    mask_x = (jnp.int32(1) << grid_levels[:, 0]) - 1
    mask_y = (jnp.int32(1) << grid_levels[:, 1]) - 1
    covered = ((row & mask_x[:, None, None]) == 0) & ((lane & mask_y[:, None, None]) == 0)
    return jnp.sum(jnp.where(covered, share[:, None, None], 0.0), axis=0)


def shifted(array, axis, by):
    size = lax.axis_size(axis)
    return lax.ppermute(array, axis, [(i, (i + by) % size) for i in range(size)])


def lead_share(offsets, index_x, index_y, size_x, size_y, tiles_across, tile_height):
    devices = size_x * size_y
    row_parts = 2 * tiles_across
    by_row = jnp.repeat(offsets[:tiles_across], 2)[:, None]
    by_col = jnp.repeat(offsets[::tiles_across], tile_height).reshape(-1, LANES)
    spread_row = jnp.broadcast_to(by_row, (row_parts, LANES))
    spread_corner = jnp.broadcast_to(offsets[0], (4, LANES))
    table = jnp.concatenate([spread_row, by_col, spread_corner], axis=0)
    owner = lax.broadcasted_iota(jnp.int32, (devices, 1, 1), 0)
    block = (owner - table[None]) % devices
    x, y = block // size_y, block % size_y
    line = lax.broadcasted_iota(jnp.int32, (1, table.shape[0], 1), 1)
    corner = line - (table.shape[0] - 4)
    shares = []
    for by in range(2):
        rows = jnp.where(y == index_y, coarse_share(x, index_x + by), 0.0)
        cols = jnp.where(x == index_x, coarse_share(y, index_y + by), 0.0)
        corners = coarse_share(x, index_x + corner // 2) * coarse_share(y, index_y + corner % 2)
        shares.append(
            jnp.where(line < row_parts, rows, jnp.where(corner < 0, cols, corners))
        )
    return jnp.stack(shares)


def local(
    owned_surplus, tile_owner, grid_levels, coefficients, faulty_grids, velocity_x, velocity_y
):
    slot_count, tile_height, tile_width = owned_surplus.shape
    rows_local, cols_local = velocity_x.shape
    size_x = lax.axis_size("gx")
    size_y = lax.axis_size("gy")
    device_count = size_x * size_y
    capacity = 2 * slot_count // device_count
    tiles_across = cols_local // tile_width
    index_x = lax.axis_index("gx")
    index_y = lax.axis_index("gy")
    own_index = index_x * size_y + index_y
    offsets = tile_owner[:slot_count]
    positions = jnp.arange(slot_count, dtype=jnp.int32)
    same_offset = offsets[:, None] == offsets[None, :]
    earlier = positions[None, :] < positions[:, None]
    slot_rank = jnp.sum((same_offset & earlier).astype(jnp.int32), axis=1)
    target = (own_index - offsets) % device_count
    source = (own_index + offsets) % device_count
    outgoing = pack(target, slot_rank, owned_surplus, device_count, capacity, tiles_across)
    incoming = lax.all_to_all(outgoing, ("gx", "gy"), split_axis=0, concat_axis=0, tiled=True)

    first_rows, last_rows, first_cols, last_cols = edges(velocity_x, velocity_y)
    speed_halo = (
        shifted(last_rows, "gx", 1),
        shifted(first_rows, "gx", -1),
        shifted(last_cols, "gy", 1),
        shifted(first_cols, "gy", -1),
    )
    incoming, speed_halo = lax.optimization_barrier((incoming, speed_halo))
    share = lead_share(offsets, index_x, index_y, size_x, size_y, tiles_across, tile_height)
    weight = weight_pattern(grid_levels, coefficients, faulty_grids)
    hat = hat_matrix(HAT).astype(jnp.bfloat16)

    nodal, first_rows, last_rows, first_cols, last_cols = refine_block(
        source, slot_rank, incoming, share, weight, hat, hat.T, rows_local, cols_local, tile_height,
        capacity,
    )
    above = shifted(last_rows, "gx", 1)
    below = shifted(first_rows, "gx", -1)
    strips = [above, below] + [side[f] for f in range(2) for side in speed_halo[:2]]
    from_left = shifted(
        jnp.concatenate([last_cols] + [strip[:, -LANES:] for strip in strips], axis=1), "gy", 1
    )
    from_right = shifted(
        jnp.concatenate([first_cols] + [strip[:, :LANES] for strip in strips], axis=1), "gy", -1
    )
    return run_steps(
        nodal, velocity_x, velocity_y, stencil_matrix(), above, below, *speed_halo, from_left, from_right
    )


def solution(mesh):
    return jax.shard_map(
        local,
        mesh=mesh,
        in_specs=(P(("gx", "gy"), None, None), P(), P(), P(), P(), P("gx", "gy"), P("gx", "gy")),
        out_specs=P("gx", "gy"),
        check_vma=False,
    )
```

profile of v0, /device:TPU:0, one launch (start us, length us, event | category | flops | bytes accessed | tf_op | source)
XLA Modules:
  0.0 110.6 jit_solution(10728140716549439986)
XLA Ops:
  0.0 0.7 and_select_fusion.2
  0.7 0.2 convert_reduce_fusion.rank_ref
  0.9 0.0 copy-start.1
  0.9 1.6 %copy-done.1 = f32[128,16,256]{2,1,0:T(8,128)S(1)} copy-done((f32[128,16,256]{2,1,0:T(8,128)S(1)}, f32[128,16,256]{2,1,0:T(8,128)}, u32[]{:S(2)}) %copy-start.1) | copy-done | bytes 2097176
  2.5 3.4 %pack_tiles.1 = f32[128,80,128]{2,1,0:T(8,128)} custom-call(s32[128]{0:T(128)S(1)} %get-tuple-element.37.target_ref, s32[128]{0:T(128)S(1)} %convert_reduce_fusion.rank_ref, f32[128,16,256]{2,1,0:T(8,128)S(1)} %copy-done.1), custom_call_target="tpu_custom_call" | custom-call | tf_op jit(solution)/shard_map/pack_tiles/pallas_call | solution.py:56
  5.9 11.6 %all-to-all-start = ((f32[128,80,128]{2,1,0:T(8,128)}), f32[128,80,128]{2,1,0:T(8,128)}, u32[]{:S(2)}, u32[]{:S(2)}) async-start(f32[128,80,128]{2,1,0:T(8,128)} %pack_tiles.1), calls=%async_computation | async-start | bytes 10485760 | tf_op jit(solution)/shard_map/all_to_all | solution.py:453
  17.5 0.0 copy-start.3
  17.5 0.0 slice-start
  17.6 0.0 copy-start.4
  17.6 0.0 copy-start.5
  17.6 0.0 copy-start.2
  17.6 2.3 %velocity_edges.1 = (f32[2,8,1024]{2,1,0:T(8,128)}, f32[2,8,1024]{2,1,0:T(8,128)}, f32[2,8,512]{2,1,0:T(8,128)}, f32[2,8,512]{2,1,0:T(8,128)}) custom-call(f32[512,1024]{1,0:T(8,128)} %x_ref.1, f32[512,1024]{1,0:T(8,128)} %x_ref.1, f32[512,1024]{1,0:T(8,128)} %x_ref.1, f32[512,1024]{1,0:T(8,128)} %x_ref.1, f32[512,1024]{1,0:T(8,128)} %y_ref.1, ...), custom_call_target="tpu_custom_call" | custom-call | tf_op jit(solution)/shard_map/velocity_edges/pallas_call | solution.py:227
  19.9 0.0 collective-permute-start
  19.9 3.0 %collective-permute-start.1 = (f32[2,8,1024]{2,1,0:T(8,128)}, f32[2,8,1024]{2,1,0:T(8,128)S(1)}, u32[]{:S(2)}, u32[]{:S(2)}) collective-permute-start(f32[2,8,1024]{2,1,0:T(8,128)} %get-tuple-element.20), channel_id=1, source_target_pairs={{0,112},{16,0},{32,16},{48,32},{64,48},{80,64},{96,80},{112,96},{1... | collective-permute-start | bytes 196616 | tf_op jit(solution)/shard_map/ppermute | solution.py:405
  22.8 1.0 collective-permute-start.2
  23.8 4.3 %collective-permute-start.3 = (f32[2,8,512]{2,1,0:T(8,128)}, f32[2,8,512]{2,1,0:T(8,128)S(1)}, u32[]{:S(2)}, u32[]{:S(2)}) collective-permute-start(f32[2,8,512]{2,1,0:T(8,128)} %get-tuple-element.22), channel_id=1, source_target_pairs={{0,15},{1,0},{2,1},{3,2},{4,3},{5,4},{6,5},{7,6},{8,7},{9,8},{10,9... | collective-permute-start | bytes 98312 | tf_op jit(solution)/shard_map/ppermute | solution.py:405
  28.2 0.1 slice.70
  28.3 0.5 slice.71
  28.8 0.1 broadcast_in_dim.108
  28.9 0.1 broadcast_in_dim.109
  29.0 0.1 broadcast_in_dim.110
  29.1 0.1 broadcast_in_dim.105
  29.1 0.1 reshape.387
  29.2 0.6 broadcast_in_dim.111
  29.9 0.1 pad.4.clone
  30.0 0.1 compare_reduce_fusion
  30.1 0.0 copy-done.2
  30.2 0.1 select_reduce_fusion.weight_ref
  30.3 0.1 add_add_fusion
  30.3 4.0 %select_select_fusion.2 = (f32[1,128,16,128]{3,2,1,0:T(8,128)S(1)}, f32[1,128,16,128]{3,2,1,0:T(8,128)S(1)}) fusion(s32[16]{0:T(128)S(1)} %get-tuple-element.60, s32[16]{0:T(128)S(1)} %get-tuple-element.61, s32[]{:T(128)S(6)} %axis_index.23, s32[]{:T(128)S(6)} %axis_index.25, s32[16,128]{1,0:T(8,128)S(1)} %add_add_fusion, ...), kind=kLoop, calls=%fused_computation.21 | loop fusion | flops 24641536 | bytes 2105520 | tf_op jit(solution)/shard_map/jit(_where)/select_n | solution.py:427
  34.3 0.1 pad_maximum_fusion.share_ref
  34.4 0.2 select_convert_fusion
  34.6 45.4 %collective-permute-done.2.speed_left = f32[2,8,512]{2,1,0:T(8,128)S(1)} collective-permute-done((f32[2,8,512]{2,1,0:T(8,128)}, f32[2,8,512]{2,1,0:T(8,128)S(1)}, u32[]{:S(2)}, u32[]{:S(2)}) %collective-permute-start.2) | collective-permute-done | bytes 32800 | tf_op jit(solution)/shard_map/ppermute | solution.py:405
  80.0 0.0 collective-permute-done.3.speed_right
  80.0 0.0 collective-permute-done.speed_above
  80.0 0.0 collective-permute-done.1.speed_below
  80.1 0.5 all-to-all-done.incoming_ref
  80.5 5.1 %refine_block.1 = (f32[8,512,128]{2,1,0:T(8,128)S(1)}, f32[8,1024]{1,0:T(8,128)S(1)}, f32[8,1024]{1,0:T(8,128)S(1)}, f32[8,512]{1,0:T(8,128)S(1)}, f32[8,512]{1,0:T(8,128)S(1)}) custom-call(s32[128]{0:T(128)S(1)} %get-tuple-element.39.source_ref, s32[128]{0:T(128)S(1)} %convert_reduce_fusion.rank_ref, f32[128,80,128]{2,1,0:T(8,128)} %all-to-all-done.incoming_ref, ...), custom_call_target="tpu_custom_call" | custom-call | tf_op jit(solution)/shard_map/refine_block/pallas_call | solution.py:182
  85.7 0.2 collective-permute-start.4
  85.9 2.8 %collective-permute-start.5 = (f32[8,1024]{1,0:T(8,128)S(1)}, f32[8,1024]{1,0:T(8,128)S(1)}, u32[]{:S(2)}, u32[]{:S(2)}) collective-permute-start(f32[8,1024]{1,0:T(8,128)S(1)} %get-tuple-element.26), channel_id=1, source_target_pairs={{0,112},{16,0},{32,16},{48,32},{64,48},{80,64},{96,80},{112,96},{1... | collective-permute-start | bytes 98312 | tf_op jit(solution)/shard_map/ppermute | solution.py:405
  88.7 1.6 %collective-permute-done.4.rows_above = f32[8,1024]{1,0:T(8,128)S(1)} collective-permute-done((f32[8,1024]{1,0:T(8,128)S(1)}, f32[8,1024]{1,0:T(8,128)S(1)}, u32[]{:S(2)}, u32[]{:S(2)}) %collective-permute-start.4) | collective-permute-done | bytes 32800 | tf_op jit(solution)/shard_map/ppermute | solution.py:405
  90.2 0.0 collective-permute-done.5.rows_below
  90.3 0.5 collective-permute-start.6
  90.8 4.9 %collective-permute-start.7 = (f32[8,1280]{1,0:T(8,128)S(1)}, f32[8,1280]{1,0:T(8,128)S(1)}, u32[]{:S(2)}, u32[]{:S(2)}) collective-permute-start(f32[8,1280]{1,0:T(8,128)S(1)} %get-tuple-element.40), channel_id=1, source_target_pairs={{0,15},{1,0},{2,1},{3,2},{4,3},{5,4},{6,5},{7,6},{8,7},{9,8},{10,9... | collective-permute-start | bytes 122888 | tf_op jit(solution)/shard_map/ppermute | solution.py:405
  95.7 0.6 fusion.11.stencil_ref
  96.4 1.3 %collective-permute-done.6.from_left = f32[8,1280]{1,0:T(8,128)S(1)} collective-permute-done((f32[8,1280]{1,0:T(8,128)S(1)}, f32[8,1280]{1,0:T(8,128)S(1)}, u32[]{:S(2)}, u32[]{:S(2)}) %collective-permute-start.6) | collective-permute-done | bytes 40992 | tf_op jit(solution)/shard_map/ppermute | solution.py:405
  97.7 0.0 collective-permute-done.7.from_right
  97.7 12.9 %heun_steps.1 = f32[512,1024]{1,0:T(8,128)} custom-call(f32[8,512,128]{2,1,0:T(8,128)S(1)} %get-tuple-element.24.nodal_ref, f32[512,1024]{1,0:T(8,128)S(1)} %copy-done, f32[512,1024]{1,0:T(8,128)} %y_ref.1, bf16[512,256]{1,0:T(8,128)(2,1)S(1)} %fusion.11.stencil_ref, f32[8,1024]{1,0:T(8,128)S(1)} %collective-permute-done.4.rows_above, ...), custom_call_target="tpu_custom_call" | custom-call | tf_op jit(solution)/shard_map/heun_steps/pallas_call | solution.py:345
  (27 shorter events, 0.1 us)
Async XLA Ops:
  0.9 1.6 %copy-start.1 = (f32[128,16,256]{2,1,0:T(8,128)S(1)}, f32[128,16,256]{2,1,0:T(8,128)}, u32[]{:S(2)}) copy-start(f32[128,16,256]{2,1,0:T(8,128)} %owned_ref.1) | copy-start | bytes 6291460
  5.9 74.6 %all-to-all-start = ((f32[128,80,128]{2,1,0:T(8,128)}), f32[128,80,128]{2,1,0:T(8,128)}, u32[]{:S(2)}, u32[]{:S(2)}) async-start(f32[128,80,128]{2,1,0:T(8,128)} %pack_tiles.1), calls=%async_computation | async-start | bytes 10485760 | tf_op jit(solution)/shard_map/all_to_all | solution.py:453
  17.5 10.7 %copy-start.3 = (s32[16384]{0:T(1024)S(1)}, s32[16384]{0:T(1024)}, u32[]{:S(2)}) copy-start(s32[16384]{0:T(1024)} %param.8) | copy-start | bytes 196612
  17.5 11.5 %slice-start = ((s32[16384]{0:T(1024)}), s32[4]{0:T(128)S(1)}, s32[]{:S(2)}) async-start(s32[16384]{0:T(1024)} %param.8), calls=%async_computation.1 | async-start | bytes 1024 | tf_op jit(solution)/shard_map/slice | solution.py:411
  17.6 12.5 %copy-start.4 = (s32[2]{0:T(128)S(1)}, s32[2]{0:T(128)}, u32[]{:S(2)}) copy-start(s32[2]{0:T(128)} %param.11) | copy-start | bytes 28
  17.6 12.6 %copy-start.5 = (s32[8]{0:T(128)S(1)}, s32[8]{0:T(128)}, u32[]{:S(2)}) copy-start(s32[8]{0:T(128)} %param.10) | copy-start | bytes 100
  17.6 12.6 %copy-start.2 = (s32[8,2]{0,1:T(2,128)S(1)}, s32[8,2]{0,1:T(2,128)}, u32[]{:S(2)}) copy-start(s32[8,2]{0,1:T(2,128)} %param.9) | copy-start | bytes 196
  19.9 60.2 %collective-permute-start = (f32[2,8,1024]{2,1,0:T(8,128)}, f32[2,8,1024]{2,1,0:T(8,128)S(1)}, u32[]{:S(2)}, u32[]{:S(2)}) collective-permute-start(f32[2,8,1024]{2,1,0:T(8,128)} %get-tuple-element.19), channel_id=1, source_target_pairs={{0,16},{16,32},{32,48},{48,64},{64,80},{80,96},{96,112},{112,0},{1... | collective-permute-start | bytes 196616 | tf_op jit(solution)/shard_map/ppermute | solution.py:405
  19.9 60.2 %collective-permute-start.1 = (f32[2,8,1024]{2,1,0:T(8,128)}, f32[2,8,1024]{2,1,0:T(8,128)S(1)}, u32[]{:S(2)}, u32[]{:S(2)}) collective-permute-start(f32[2,8,1024]{2,1,0:T(8,128)} %get-tuple-element.20), channel_id=1, source_target_pairs={{0,112},{16,0},{32,16},{48,32},{64,48},{80,64},{96,80},{112,96},{1... | collective-permute-start | bytes 196616 | tf_op jit(solution)/shard_map/ppermute | solution.py:405
  22.8 57.2 %collective-permute-start.2 = (f32[2,8,512]{2,1,0:T(8,128)}, f32[2,8,512]{2,1,0:T(8,128)S(1)}, u32[]{:S(2)}, u32[]{:S(2)}) collective-permute-start(f32[2,8,512]{2,1,0:T(8,128)} %get-tuple-element.21), channel_id=1, source_target_pairs={{0,1},{1,2},{2,3},{3,4},{4,5},{5,6},{6,7},{7,8},{8,9},{9,10},{10,1... | collective-permute-start | bytes 98312 | tf_op jit(solution)/shard_map/ppermute | solution.py:405
  23.8 56.2 %collective-permute-start.3 = (f32[2,8,512]{2,1,0:T(8,128)}, f32[2,8,512]{2,1,0:T(8,128)S(1)}, u32[]{:S(2)}, u32[]{:S(2)}) collective-permute-start(f32[2,8,512]{2,1,0:T(8,128)} %get-tuple-element.22), channel_id=1, source_target_pairs={{0,15},{1,0},{2,1},{3,2},{4,3},{5,4},{6,5},{7,6},{8,7},{9,8},{10,9... | collective-permute-start | bytes 98312 | tf_op jit(solution)/shard_map/ppermute | solution.py:405
  80.5 17.1 %copy-start = (f32[512,1024]{1,0:T(8,128)S(1)}, f32[512,1024]{1,0:T(8,128)}, u32[]{:S(2)}) copy-start(f32[512,1024]{1,0:T(8,128)} %x_ref.1) | copy-start | bytes 6291460
  85.7 4.6 %collective-permute-start.4 = (f32[8,1024]{1,0:T(8,128)S(1)}, f32[8,1024]{1,0:T(8,128)S(1)}, u32[]{:S(2)}, u32[]{:S(2)}) collective-permute-start(f32[8,1024]{1,0:T(8,128)S(1)} %get-tuple-element.25), channel_id=1, source_target_pairs={{0,16},{16,32},{32,48},{48,64},{64,80},{80,96},{96,112},{112,0},{1... | collective-permute-start | bytes 98312 | tf_op jit(solution)/shard_map/ppermute | solution.py:405
  85.9 4.4 %collective-permute-start.5 = (f32[8,1024]{1,0:T(8,128)S(1)}, f32[8,1024]{1,0:T(8,128)S(1)}, u32[]{:S(2)}, u32[]{:S(2)}) collective-permute-start(f32[8,1024]{1,0:T(8,128)S(1)} %get-tuple-element.26), channel_id=1, source_target_pairs={{0,112},{16,0},{32,16},{48,32},{64,48},{80,64},{96,80},{112,96},{1... | collective-permute-start | bytes 98312 | tf_op jit(solution)/shard_map/ppermute | solution.py:405
  90.3 7.4 %collective-permute-start.6 = (f32[8,1280]{1,0:T(8,128)S(1)}, f32[8,1280]{1,0:T(8,128)S(1)}, u32[]{:S(2)}, u32[]{:S(2)}) collective-permute-start(f32[8,1280]{1,0:T(8,128)S(1)} %get-tuple-element.41), channel_id=1, source_target_pairs={{0,1},{1,2},{2,3},{3,4},{4,5},{5,6},{6,7},{7,8},{8,9},{9,10},{10,1... | collective-permute-start | bytes 122888 | tf_op jit(solution)/shard_map/ppermute | solution.py:405
  90.8 6.9 %collective-permute-start.7 = (f32[8,1280]{1,0:T(8,128)S(1)}, f32[8,1280]{1,0:T(8,128)S(1)}, u32[]{:S(2)}, u32[]{:S(2)}) collective-permute-start(f32[8,1280]{1,0:T(8,128)S(1)} %get-tuple-element.40), channel_id=1, source_target_pairs={{0,15},{1,0},{2,1},{3,2},{4,3},{5,4},{6,5},{7,6},{8,7},{9,8},{10,9... | collective-permute-start | bytes 122888 | tf_op jit(solution)/shard_map/ppermute | solution.py:405
where the time goes:
time: 111 us
  waiting for transfers between devices  48.8 us (44%)
  starting transfers between devices  28.3 us (25%)
  Pallas kernels  23.7 us (21%)
  other arithmetic  6.11 us (6%)
  local copies, waits for them, and re-layouts  3.42 us (3%)
    ppermute x8, waiting for transfers between devices, shifted(): lax.ppermute(array, axis, [(i, (i + by) % size) for i in range(size)])  48.3 us
    ppermute x8, starting transfers between devices, shifted(): lax.ppermute(array, axis, [(i, (i + by) % size) for i in range(size)])  16.7 us
    pallas_call x1, Pallas kernels, run_steps(): pl.pallas_call(functools.partial(steps_kernel, largest_chunk(height + 2 *...  12.9 us
    all_to_all x1, starting transfers between devices, local(): lax.all_to_all(outgoing, ('gx', 'gy'), split_axis=0, concat_axis=0, tiled...  11.6 us
    pallas_call x1, Pallas kernels, refine_block(): pl.pallas_call(functools.partial(refine_kernel, width // HAT, tile_rows,...  5.12 us
    select_n x1, other arithmetic, lead_share(): jnp.where(line < row_parts, rows, jnp.where(corner < 0, cols, corners))  3.95 us
    pallas_call x1, Pallas kernels, pack(): pl.pallas_call(functools.partial(pack_kernel, tiles_across, capacity), ou...  3.44 us
    pallas_call x1, Pallas kernels, edges(): pl.pallas_call(edges_kernel, grid=(1,), out_shape=[jax.ShapeDtypeStruct(s...  2.26 us
  transfers between devices with their start and end apart: 9, of which 4 were waited for; matrix products, arithmetic and copies ran while one was open for 6% of the time, Pallas kernels for 2%

commit v1 on v0

--- a/solution.py
+++ b/solution.py
@@ -14,55 +14,102 @@
 LANES = 128
 HAT = 256
 VMEM_LIMIT = 48 << 20
-
-
-def pack_kernel(tiles_across, capacity, target_ref, rank_ref, owned_ref, outgoing_ref):
+PACK_LIMIT = 60 << 20
+
+
+def pack_kernel(
+    tiles_across, capacity, owner_ref, owned_ref, outgoing_ref, staged, wide, leads, offsets, used,
+    sem_in, sem_out, sem_lead, sem_owner,
+):
     count, tile_rows, _ = owned_ref.shape
     messages = outgoing_ref.shape[0]
-    half = tile_rows
+    size = 2 * tile_rows
+    groups = sem_in.shape[0]
+    per_group = count // groups
+
+    def arrival(g):
+        part = pl.ds(g * per_group, per_group)
+        return pltpu.make_async_copy(owned_ref.at[part], staged.at[part], sem_in.at[g])
+
+    head = pltpu.make_async_copy(owner_ref.at[pl.ds(0, count)], offsets, sem_owner)
+    head.start()
+    for g in range(groups):
+        arrival(g).start()
+    own_index = lax.axis_index("gx") * lax.axis_size("gy") + lax.axis_index("gy")
+
+    def clear(m, carry):
+        used[m] = 0
+        return carry
+
+    lax.fori_loop(0, messages, clear, 0, unroll=8)
+    head.wait()
+    for g in range(groups):
+        arrival(g).wait()
+
+        def place(i, carry, g=g):
+            k = g * per_group + i
+            wide[k, :tile_rows, :] = staged[k, :, :LANES]
+            wide[k, tile_rows:, :] = staged[k, :, LANES:]
+            offset = offsets[k]
+            rank = used[offset]
+            used[offset] = rank + 1
+            target = lax.rem(own_index - offset + messages, messages)
+            row = pl.multiple_of(rank * size, size)
+            pltpu.make_async_copy(
+                wide.at[k], outgoing_ref.at[target, pl.ds(row, size), :], sem_out
+            ).start()
+            return carry
+
+        lax.fori_loop(0, per_group, place, 0, unroll=8)
+
     rows = []
     for ky in range(tiles_across):
-        rows += [owned_ref[ky, 0:1, :LANES], owned_ref[ky, 0:1, LANES:]]
+        rows += [staged[ky, 0:1, :LANES], staged[ky, 0:1, LANES:]]
     per_part = LANES // tile_rows
     for part in range(count // tiles_across // per_part):
-        columns = [
-            owned_ref[(part * per_part + t) * tiles_across, :, :LANES] for t in range(per_part)
-        ]
+        columns = [staged[(part * per_part + t) * tiles_across, :, :LANES] for t in range(per_part)]
         rows.append(jnp.concatenate(columns, axis=0).T[0:1])
     rows += [rows[0]] * 4
     lead = jnp.concatenate(rows, axis=0)
 
     def address(m, carry):
-        outgoing_ref[m, pl.ds(2 * half * capacity, lead.shape[0]), :] = lead
+        leads[m] = lead
         return carry
 
     lax.fori_loop(0, messages, address, 0, unroll=8)
-
-    def place(k, carry):
-        m = target_ref[k]
-        row = pl.multiple_of(rank_ref[k] * (2 * half), 2 * half)
-        outgoing_ref[m, pl.ds(row, half), :] = owned_ref[k, :, :LANES]
-        outgoing_ref[m, pl.ds(row + half, half), :] = owned_ref[k, :, LANES:]
-        return carry
-
-    lax.fori_loop(0, count, place, 0, unroll=8)
-
-
-def pack(target, rank, owned, messages, capacity, tiles_across):
+    to_all = pltpu.make_async_copy(
+        leads, outgoing_ref.at[:, pl.ds(size * capacity, lead.shape[0]), :], sem_lead
+    )
+    to_all.start()
+    to_all.wait()
+    pltpu.make_async_copy(wide, wide, sem_out).wait()
+
+
+def pack(tile_owner, owned, messages, capacity, tiles_across):
     count, tile_rows, _ = owned.shape
     lead_rows = 2 * tiles_across + count // tiles_across * tile_rows // LANES + 4
-    smem = pl.BlockSpec(memory_space=pltpu.SMEM)
-    vmem = pl.BlockSpec(memory_space=pltpu.VMEM)
+    anywhere = pl.BlockSpec(memory_space=pl.ANY)
     return pl.pallas_call(
         functools.partial(pack_kernel, tiles_across, capacity),
         out_shape=jax.ShapeDtypeStruct(
             (messages, capacity * tile_rows * 2 + lead_rows, LANES), owned.dtype
         ),
-        in_specs=[smem, smem, vmem],
-        out_specs=vmem,
-        compiler_params=pltpu.CompilerParams(vmem_limit_bytes=VMEM_LIMIT),
+        in_specs=[anywhere, anywhere],
+        out_specs=anywhere,
+        scratch_shapes=[
+            pltpu.VMEM(owned.shape, owned.dtype),
+            pltpu.VMEM((count, 2 * tile_rows, LANES), owned.dtype),
+            pltpu.VMEM((messages, lead_rows, LANES), owned.dtype),
+            pltpu.SMEM((count,), jnp.int32),
+            pltpu.SMEM((messages,), jnp.int32),
+            pltpu.SemaphoreType.DMA((8,)),
+            pltpu.SemaphoreType.DMA,
+            pltpu.SemaphoreType.DMA,
+            pltpu.SemaphoreType.DMA,
+        ],
+        compiler_params=pltpu.CompilerParams(vmem_limit_bytes=PACK_LIMIT),
         name="pack_tiles",
-    )(target, rank, owned)
+    )(tile_owner, owned)
 
 
 def split_dot(left, right, split_left):
@@ -79,7 +126,7 @@
 def refine_kernel(
     tiles_across, tile_rows, capacity, source_ref, rank_ref, incoming_ref, share_ref, weight_ref,
     hat_x_ref, hat_y_ref, nodal_ref, first_rows_ref, last_rows_ref, left_ref, right_ref,
-    block, edge,
+    block, edge, staged, leads, sem_tile, sem_lead,
 ):
     height = nodal_ref.shape[1]
     tiles_down = height // tile_rows
@@ -88,26 +135,32 @@
     lead_row = 2 * tile_rows * capacity
     lead_size = share_ref.shape[2]
     tile_weight = jnp.concatenate([weight_ref[...]] * (tile_rows // 8), axis=0)
-
-    def place(kx, carry):
-        row = pl.multiple_of(kx * tile_rows, tile_rows)
-        for ky in range(tiles_across):
-            message = source_ref[kx * tiles_across + ky]
-            start = pl.multiple_of(rank_ref[kx * tiles_across + ky] * (2 * tile_rows), 2 * tile_rows)
-            for part in range(2):
-                block[pl.ds(row, tile_rows), (2 * ky + part) * LANES : (2 * ky + part + 1) * LANES] = (
-                    incoming_ref[message, pl.ds(start + part * tile_rows, tile_rows), :] * tile_weight
-                )
-        return carry
-
-    lax.fori_loop(0, tiles_down, place, 0, unroll=2)
+    size = 2 * tile_rows
+    groups = sem_tile.shape[0]
+    per_group = tiles_down * tiles_across // groups
+    lead_copy = pltpu.make_async_copy(
+        incoming_ref.at[:, pl.ds(lead_row, lead_size), :], leads, sem_lead
+    )
+    lead_copy.start()
+    for g in range(groups):
+
+        def fetch(i, carry, g=g):
+            k = g * per_group + i
+            row = pl.multiple_of(rank_ref[k] * size, size)
+            pltpu.make_async_copy(
+                incoming_ref.at[source_ref[k], pl.ds(row, size), :], staged.at[k], sem_tile.at[g]
+            ).start()
+            return carry
+
+        lax.fori_loop(0, per_group, fetch, 0, unroll=8)
+    lead_copy.wait()
 
     def collect(m, sums):
-        lead = incoming_ref[m, pl.ds(lead_row, lead_size), :]
+        lead = leads[m]
         return tuple(total + share_ref[i, m] * lead for i, total in enumerate(sums))
 
     zero = jnp.zeros((lead_size, LANES), jnp.float32)
-    own_lead, next_lead = lax.fori_loop(0, incoming_ref.shape[0], collect, (zero, zero), unroll=8)
+    own_lead, next_lead = lax.fori_loop(0, leads.shape[0], collect, (zero, zero), unroll=8)
 
     weight = weight_ref[...]
     lane = lax.broadcasted_iota(jnp.int32, (1, LANES), 1)
@@ -144,6 +197,23 @@
             target[rows, lanes] = split_dot(hat_x_ref[...], values, False) + ramp_rows[:, :width] * last
 
     refine_down(edge, slice(0, LANES), corner(0), corner(1))
+
+    def place(kx, carry):
+        row = pl.multiple_of(kx * tile_rows, tile_rows)
+        for ky in range(tiles_across):
+            for part in range(2):
+                block[pl.ds(row, tile_rows), (2 * ky + part) * LANES : (2 * ky + part + 1) * LANES] = (
+                    staged[kx * tiles_across + ky, part * tile_rows : (part + 1) * tile_rows, :]
+                    * tile_weight
+                )
+        return carry
+
+    for g in range(groups):
+        part = staged.at[pl.ds(g * per_group, per_group)]
+        pltpu.make_async_copy(part, part, sem_tile.at[g]).wait()
+        lax.fori_loop(
+            g * tiles_down // groups, (g + 1) * tiles_down // groups, place, 0, unroll=2
+        )
     line = lambda lead, ky: (
         jnp.concatenate([lead[2 * ky : 2 * ky + 1], lead[2 * ky + 1 : 2 * ky + 2]], axis=1)
         * jnp.concatenate([weight[0:1]] * 2, axis=1)
@@ -182,10 +252,15 @@
     return pl.pallas_call(
         functools.partial(refine_kernel, width // HAT, tile_rows, capacity),
         out_shape=[jax.ShapeDtypeStruct(shape, jnp.float32) for shape in shapes],
-        in_specs=[smem, smem] + [vmem] * 5,
+        in_specs=[smem, smem, pl.BlockSpec(memory_space=pltpu.HBM)] + [vmem] * 4,
         out_specs=[vmem] * len(shapes),
         scratch_shapes=[
-            pltpu.VMEM((height, width), jnp.float32), pltpu.VMEM((height, LANES), jnp.float32)
+            pltpu.VMEM((height, width), jnp.float32),
+            pltpu.VMEM((height, LANES), jnp.float32),
+            pltpu.VMEM((source.shape[0], 2 * tile_rows, LANES), jnp.float32),
+            pltpu.VMEM((incoming.shape[0], share.shape[2], LANES), jnp.float32),
+            pltpu.SemaphoreType.DMA((4,)),
+            pltpu.SemaphoreType.DMA,
         ],
         compiler_params=pltpu.CompilerParams(vmem_limit_bytes=VMEM_LIMIT),
         name="refine_block",
@@ -236,7 +311,7 @@
 
 def steps_kernel(
     chunk, last_chunk, nodal_ref, x_ref, y_ref, stencil_ref, rows_above, rows_below, speed_above,
-    speed_below, speed_left, speed_right, from_left, from_right, out_ref, field, middle, speed,
+    speed_below, speed_left, speed_right, from_left, from_right, out_ref, field, middle, speed, result_ref, sem,
 ):
     tiles, height, _ = nodal_ref.shape
     width = tiles * LANES
@@ -285,16 +360,14 @@
                 stencil_ref[...],
                 preferred_element_type=jnp.float32,
             )
-            here = source[t, pl.ds(start, size), :]
             one_below = source[t, pl.ds(start - 1, size), :]
             one_above = source[t, pl.ds(start + 1, size), :]
             two_below = source[t, pl.ds(start - 2, size), :]
             two_above = source[t, pl.ds(start + 2, size), :]
             curve = 16.0 * (one_above + one_below) - (two_above + two_below) + across[:, :LANES]
             slope = 8.0 * (one_above - one_below) - (two_above - two_below)
-            change = scale * curve - speed[0, t, pl.ds(start, size), :] * slope
-            change = change - speed[1, t, pl.ds(start, size), :] * across[:, LANES:]
-            store(t, (1.0 - 60.0 * scale) * here + change)
+            result = scale * curve - speed[0, t, pl.ds(start, size), :] * slope
+            store(t, result - speed[1, t, pl.ds(start, size), :] * across[:, LANES:])
 
     def first_half(c, carry):
         start = pl.multiple_of(HALO + c * chunk, HALO)
@@ -319,11 +392,13 @@
         place = pl.multiple_of(c * last_chunk, HALO)
 
         def store(t, result):
-            out_ref[pl.ds(place, last_chunk), t * LANES : (t + 1) * LANES] = 0.5 * (
+            result_ref[pl.ds(place, last_chunk), t * LANES : (t + 1) * LANES] = 0.5 * (
                 field[t, pl.ds(start, last_chunk), :] + result
             )
 
         advance(middle, start, last_chunk, range(tiles), store)
+        rows = pl.ds(place, last_chunk)
+        pltpu.make_async_copy(result_ref.at[rows], out_ref.at[rows], sem).start()
         return carry
 
     extended = (height + 2 * HALO) // chunk
@@ -332,6 +407,7 @@
         if step < STEPS - 1:
             lax.fori_loop(0, extended, second_half, 0)
     lax.fori_loop(0, height // last_chunk, last_half, 0)
+    pltpu.make_async_copy(result_ref, out_ref, sem).wait()
 
 
 def largest_chunk(rows, limit):
@@ -348,11 +424,13 @@
         ),
         out_shape=jax.ShapeDtypeStruct((height, tiles * LANES), jnp.float32),
         in_specs=[vmem] * (4 + len(halo)),
-        out_specs=vmem,
+        out_specs=pl.BlockSpec(memory_space=pl.ANY),
         scratch_shapes=[
             pltpu.VMEM(extended, jnp.float32),
             pltpu.VMEM(extended, jnp.float32),
             pltpu.VMEM((2,) + extended, jnp.float32),
+            pltpu.VMEM((height, tiles * LANES), jnp.float32),
+            pltpu.SemaphoreType.DMA,
         ],
         compiler_params=pltpu.CompilerParams(vmem_limit_bytes=VMEM_LIMIT),
         name="heun_steps",
@@ -366,7 +444,9 @@
     outside = jnp.where(lane < LANES // 2, lane + LANES, lane - LANES)
     shift = jnp.where(row < 2 * LANES, lane, outside) - column % LANES
     distance = jnp.abs(shift)
+    centre = 12.0 / (TIME_STEP * DIFFUSION) - 60.0
     curve = jnp.where(distance == 1, 16.0, jnp.where(distance == 2, -1.0, 0.0))
+    curve = jnp.where(distance == 0, centre, curve)
     slope = jnp.where(distance == 1, 8.0, jnp.where(distance == 2, -1.0, 0.0)) * jnp.sign(
         shift
     ).astype(jnp.float32)
@@ -447,9 +527,8 @@
     same_offset = offsets[:, None] == offsets[None, :]
     earlier = positions[None, :] < positions[:, None]
     slot_rank = jnp.sum((same_offset & earlier).astype(jnp.int32), axis=1)
-    target = (own_index - offsets) % device_count
     source = (own_index + offsets) % device_count
-    outgoing = pack(target, slot_rank, owned_surplus, device_count, capacity, tiles_across)
+    outgoing = pack(tile_owner, owned_surplus, device_count, capacity, tiles_across)
     incoming = lax.all_to_all(outgoing, ("gx", "gy"), split_axis=0, concat_axis=0, tiled=True)
 
     first_rows, last_rows, first_cols, last_cols = edges(velocity_x, velocity_y)

time: 111 us -> 107 us (0.964)
  Pallas kernels: 23.7 us -> 21.7 us
  local copies, waits for them, and re-layouts: 3.42 us -> 1.81 us
    unnamed x19 -> x17, local copies, waits for them, and re-layouts: 1.64 us -> 0.05 us
    pallas_call x1, Pallas kernels: 12.9 us -> 11.8 us  [run_steps(): pl.pallas_call(functools.partial(steps_kernel, largest_chunk(height + 2 *...]
  transfers between devices with their start and end apart: 9 -> 9, of which waited for: 4 -> 4; matrix products, arithmetic and copies ran while one was open for 6% -> 7% of each run, Pallas kernels for 2% -> 2%
where the time goes in v1:
time: 107 us; the launch traced here: 106 us
  waiting for transfers between devices  48.6 us (45%)
  starting transfers between devices  28.3 us (26%)
  Pallas kernels  21.7 us (20%)
  other arithmetic  5.43 us (5%)
  local copies, waits for them, and re-layouts  1.81 us (2%)
    ppermute x8, waiting for transfers between devices, shifted(): lax.ppermute(array, axis, [(i, (i + by) % size) for i in range(size)])  48.1 us
    ppermute x8, starting transfers between devices, shifted(): lax.ppermute(array, axis, [(i, (i + by) % size) for i in range(size)])  16.7 us
    pallas_call x1, Pallas kernels, run_steps(): pl.pallas_call(functools.partial(steps_kernel, largest_chunk(height + 2 *...  11.8 us
    all_to_all x1, starting transfers between devices, local(): lax.all_to_all(outgoing, ('gx', 'gy'), split_axis=0, concat_axis=0, tiled...  11.6 us
    pallas_call x1, Pallas kernels, refine_block(): pl.pallas_call(functools.partial(refine_kernel, width // HAT, tile_rows,...  4.33 us
    select_n x1, other arithmetic, lead_share(): jnp.where(line < row_parts, rows, jnp.where(corner < 0, cols, corners))  3.95 us
    pallas_call x1, Pallas kernels, pack(): pl.pallas_call(functools.partial(pack_kernel, tiles_across, capacity), ou...  3.32 us
    pallas_call x1, Pallas kernels, edges(): pl.pallas_call(edges_kernel, grid=(1,), out_shape=[jax.ShapeDtypeStruct(s...  2.25 us
  transfers between devices with their start and end apart: 9, of which 4 were waited for; matrix products, arithmetic and copies ran while one was open for 7% of the time, Pallas kernels for 2%

profile of v1, /device:TPU:0, one launch (start us, length us, event | category | flops | bytes accessed | tf_op | source)
XLA Modules:
  0.0 106.3 jit_solution(901573497008852628)
XLA Ops:
  0.0 3.3 %pack_tiles.1 = f32[128,80,128]{2,1,0:T(8,128)} custom-call(s32[16384]{0:T(1024)} %owner_ref.1, f32[128,16,256]{2,1,0:T(8,128)} %owned_ref.1), custom_call_target="tpu_custom_call" | custom-call | tf_op jit(solution)/shard_map/pack_tiles/pallas_call | solution.py:92
  3.3 11.6 %all-to-all-start = ((f32[128,80,128]{2,1,0:T(8,128)}), f32[128,80,128]{2,1,0:T(8,128)}, u32[]{:S(2)}, u32[]{:S(2)}) async-start(f32[128,80,128]{2,1,0:T(8,128)} %pack_tiles.1), calls=%async_computation | async-start | bytes 10485760 | tf_op jit(solution)/shard_map/all_to_all | solution.py:532
  15.0 0.0 copy-start.1
  15.0 0.0 slice-start
  15.0 0.0 copy-start.3
  15.0 0.0 copy-start.4
  15.0 0.0 copy-start.2
  15.0 2.2 %velocity_edges.1 = (f32[2,8,1024]{2,1,0:T(8,128)}, f32[2,8,1024]{2,1,0:T(8,128)}, f32[2,8,512]{2,1,0:T(8,128)}, f32[2,8,512]{2,1,0:T(8,128)}) custom-call(f32[512,1024]{1,0:T(8,128)} %x_ref.1, f32[512,1024]{1,0:T(8,128)} %x_ref.1, f32[512,1024]{1,0:T(8,128)} %x_ref.1, f32[512,1024]{1,0:T(8,128)} %x_ref.1, f32[512,1024]{1,0:T(8,128)} %y_ref.1, ...), custom_call_target="tpu_custom_call" | custom-call | tf_op jit(solution)/shard_map/velocity_edges/pallas_call | solution.py:302
  17.3 0.0 collective-permute-start
  17.3 3.0 %collective-permute-start.1 = (f32[2,8,1024]{2,1,0:T(8,128)}, f32[2,8,1024]{2,1,0:T(8,128)S(1)}, u32[]{:S(2)}, u32[]{:S(2)}) collective-permute-start(f32[2,8,1024]{2,1,0:T(8,128)} %get-tuple-element.20), channel_id=1, source_target_pairs={{0,112},{16,0},{32,16},{48,32},{64,48},{80,64},{96,80},{112,96},{1... | collective-permute-start | bytes 196616 | tf_op jit(solution)/shard_map/ppermute | solution.py:485
  20.2 1.0 collective-permute-start.2
  21.2 4.3 %collective-permute-start.3 = (f32[2,8,512]{2,1,0:T(8,128)}, f32[2,8,512]{2,1,0:T(8,128)S(1)}, u32[]{:S(2)}, u32[]{:S(2)}) collective-permute-start(f32[2,8,512]{2,1,0:T(8,128)} %get-tuple-element.22), channel_id=1, source_target_pairs={{0,15},{1,0},{2,1},{3,2},{4,3},{5,4},{6,5},{7,6},{8,7},{9,8},{10,9... | collective-permute-start | bytes 98312 | tf_op jit(solution)/shard_map/ppermute | solution.py:485
  25.6 0.0 copy-done.1
  25.6 0.5 slice.71
  26.1 0.1 slice.70
  26.2 0.1 broadcast_in_dim.111
  26.3 0.1 broadcast_in_dim.112
  26.4 0.1 broadcast_in_dim.113
  26.5 0.0 slice-done
  26.5 0.1 broadcast_in_dim.108
  26.5 0.1 reshape.387
  26.6 0.6 broadcast_in_dim.114
  27.3 0.1 pad.4.clone
  27.4 0.0 copy-done.3
  27.4 0.1 compare_reduce_fusion
  27.5 0.2 convert_reduce_fusion.rank_ref
  27.7 0.0 copy-done.4
  27.8 0.1 select_reduce_fusion.weight_ref
  27.9 0.1 add_add_fusion
  27.9 4.0 %select_select_fusion.2 = (f32[1,128,16,128]{3,2,1,0:T(8,128)S(1)}, f32[1,128,16,128]{3,2,1,0:T(8,128)S(1)}) fusion(s32[16]{0:T(128)S(1)} %get-tuple-element.59, s32[16]{0:T(128)S(1)} %get-tuple-element.60, s32[]{:T(128)S(6)} %axis_index.23, s32[]{:T(128)S(6)} %axis_index.25, s32[16,128]{1,0:T(8,128)S(1)} %add_add_fusion, ...), kind=kLoop, calls=%fused_computation.21 | loop fusion | flops 24641536 | bytes 2105520 | tf_op jit(solution)/shard_map/jit(_where)/select_n | solution.py:507
  31.9 0.1 pad_maximum_fusion.share_ref
  32.0 0.2 select_convert_fusion
  32.2 45.2 %collective-permute-done.2.speed_left = f32[2,8,512]{2,1,0:T(8,128)S(1)} collective-permute-done((f32[2,8,512]{2,1,0:T(8,128)}, f32[2,8,512]{2,1,0:T(8,128)S(1)}, u32[]{:S(2)}, u32[]{:S(2)}) %collective-permute-start.2) | collective-permute-done | bytes 32800 | tf_op jit(solution)/shard_map/ppermute | solution.py:485
  77.5 0.0 collective-permute-done.3.speed_right
  77.5 0.0 collective-permute-done.speed_above
  77.5 0.0 collective-permute-done.1.speed_below
  77.5 0.5 all-to-all-done.incoming_ref
  78.0 4.3 %refine_block.1 = (f32[8,512,128]{2,1,0:T(8,128)S(1)}, f32[8,1024]{1,0:T(8,128)S(1)}, f32[8,1024]{1,0:T(8,128)S(1)}, f32[8,512]{1,0:T(8,128)S(1)}, f32[8,512]{1,0:T(8,128)S(1)}) custom-call(s32[128]{0:T(128)S(1)} %get-tuple-element.38.source_ref, s32[128]{0:T(128)S(1)} %convert_reduce_fusion.rank_ref, f32[128,80,128]{2,1,0:T(8,128)} %all-to-all-done.incoming_ref, ...), custom_call_target="tpu_custom_call" | custom-call | tf_op jit(solution)/shard_map/refine_block/pallas_call | solution.py:252
  82.3 0.2 collective-permute-start.4
  82.5 2.8 %collective-permute-start.5 = (f32[8,1024]{1,0:T(8,128)S(1)}, f32[8,1024]{1,0:T(8,128)S(1)}, u32[]{:S(2)}, u32[]{:S(2)}) collective-permute-start(f32[8,1024]{1,0:T(8,128)S(1)} %get-tuple-element.26), channel_id=1, source_target_pairs={{0,112},{16,0},{32,16},{48,32},{64,48},{80,64},{96,80},{112,96},{1... | collective-permute-start | bytes 98312 | tf_op jit(solution)/shard_map/ppermute | solution.py:485
  85.3 1.6 %collective-permute-done.4.rows_above = f32[8,1024]{1,0:T(8,128)S(1)} collective-permute-done((f32[8,1024]{1,0:T(8,128)S(1)}, f32[8,1024]{1,0:T(8,128)S(1)}, u32[]{:S(2)}, u32[]{:S(2)}) %collective-permute-start.4) | collective-permute-done | bytes 32800 | tf_op jit(solution)/shard_map/ppermute | solution.py:485
  86.9 0.0 collective-permute-done.5.rows_below
  86.9 0.5 collective-permute-start.6
  87.4 4.9 %collective-permute-start.7 = (f32[8,1280]{1,0:T(8,128)S(1)}, f32[8,1280]{1,0:T(8,128)S(1)}, u32[]{:S(2)}, u32[]{:S(2)}) collective-permute-start(f32[8,1280]{1,0:T(8,128)S(1)} %get-tuple-element.39), channel_id=1, source_target_pairs={{0,15},{1,0},{2,1},{3,2},{4,3},{5,4},{6,5},{7,6},{8,7},{9,8},{10,9... | collective-permute-start | bytes 122888 | tf_op jit(solution)/shard_map/ppermute | solution.py:485
  92.3 0.7 fusion.12.stencil_ref
  93.0 1.3 %collective-permute-done.6.from_left = f32[8,1280]{1,0:T(8,128)S(1)} collective-permute-done((f32[8,1280]{1,0:T(8,128)S(1)}, f32[8,1280]{1,0:T(8,128)S(1)}, u32[]{:S(2)}, u32[]{:S(2)}) %collective-permute-start.6) | collective-permute-done | bytes 40992 | tf_op jit(solution)/shard_map/ppermute | solution.py:485
  94.3 0.0 collective-permute-done.7.from_right
  94.3 11.8 %heun_steps.1 = f32[512,1024]{1,0:T(8,128)} custom-call(f32[8,512,128]{2,1,0:T(8,128)S(1)} %get-tuple-element.24.nodal_ref, f32[512,1024]{1,0:T(8,128)S(1)} %copy-done, f32[512,1024]{1,0:T(8,128)} %y_ref.1, bf16[512,256]{1,0:T(8,128)(2,1)S(1)} %fusion.12.stencil_ref, f32[8,1024]{1,0:T(8,128)S(1)} %collective-permute-done.4.rows_above, ...), custom_call_target="tpu_custom_call" | custom-call | tf_op jit(solution)/shard_map/heun_steps/pallas_call | solution.py:421
  (25 shorter events, 0.1 us)
Async XLA Ops:
  3.3 74.6 %all-to-all-start = ((f32[128,80,128]{2,1,0:T(8,128)}), f32[128,80,128]{2,1,0:T(8,128)}, u32[]{:S(2)}, u32[]{:S(2)}) async-start(f32[128,80,128]{2,1,0:T(8,128)} %pack_tiles.1), calls=%async_computation | async-start | bytes 10485760 | tf_op jit(solution)/shard_map/all_to_all | solution.py:532
  15.0 10.6 %copy-start.1 = (s32[16384]{0:T(1024)S(1)}, s32[16384]{0:T(1024)}, u32[]{:S(2)}) copy-start(s32[16384]{0:T(1024)} %owner_ref.1) | copy-start | bytes 196612
  15.0 11.5 %slice-start = ((s32[16384]{0:T(1024)}), s32[4]{0:T(128)S(1)}, s32[]{:S(2)}) async-start(s32[16384]{0:T(1024)} %owner_ref.1), calls=%async_computation.1 | async-start | bytes 1024 | tf_op jit(solution)/shard_map/slice | solution.py:491
  15.0 12.5 %copy-start.3 = (s32[2]{0:T(128)S(1)}, s32[2]{0:T(128)}, u32[]{:S(2)}) copy-start(s32[2]{0:T(128)} %param.11) | copy-start | bytes 28
  15.0 12.7 %copy-start.4 = (s32[8]{0:T(128)S(1)}, s32[8]{0:T(128)}, u32[]{:S(2)}) copy-start(s32[8]{0:T(128)} %param.10) | copy-start | bytes 100
  15.0 12.7 %copy-start.2 = (s32[8,2]{0,1:T(2,128)S(1)}, s32[8,2]{0,1:T(2,128)}, u32[]{:S(2)}) copy-start(s32[8,2]{0,1:T(2,128)} %param.9) | copy-start | bytes 196
  17.3 60.2 %collective-permute-start = (f32[2,8,1024]{2,1,0:T(8,128)}, f32[2,8,1024]{2,1,0:T(8,128)S(1)}, u32[]{:S(2)}, u32[]{:S(2)}) collective-permute-start(f32[2,8,1024]{2,1,0:T(8,128)} %get-tuple-element.19), channel_id=1, source_target_pairs={{0,16},{16,32},{32,48},{48,64},{64,80},{80,96},{96,112},{112,0},{1... | collective-permute-start | bytes 196616 | tf_op jit(solution)/shard_map/ppermute | solution.py:485
  17.3 60.2 %collective-permute-start.1 = (f32[2,8,1024]{2,1,0:T(8,128)}, f32[2,8,1024]{2,1,0:T(8,128)S(1)}, u32[]{:S(2)}, u32[]{:S(2)}) collective-permute-start(f32[2,8,1024]{2,1,0:T(8,128)} %get-tuple-element.20), channel_id=1, source_target_pairs={{0,112},{16,0},{32,16},{48,32},{64,48},{80,64},{96,80},{112,96},{1... | collective-permute-start | bytes 196616 | tf_op jit(solution)/shard_map/ppermute | solution.py:485
  20.2 57.2 %collective-permute-start.2 = (f32[2,8,512]{2,1,0:T(8,128)}, f32[2,8,512]{2,1,0:T(8,128)S(1)}, u32[]{:S(2)}, u32[]{:S(2)}) collective-permute-start(f32[2,8,512]{2,1,0:T(8,128)} %get-tuple-element.21), channel_id=1, source_target_pairs={{0,1},{1,2},{2,3},{3,4},{4,5},{5,6},{6,7},{7,8},{8,9},{9,10},{10,1... | collective-permute-start | bytes 98312 | tf_op jit(solution)/shard_map/ppermute | solution.py:485
  21.2 56.2 %collective-permute-start.3 = (f32[2,8,512]{2,1,0:T(8,128)}, f32[2,8,512]{2,1,0:T(8,128)S(1)}, u32[]{:S(2)}, u32[]{:S(2)}) collective-permute-start(f32[2,8,512]{2,1,0:T(8,128)} %get-tuple-element.22), channel_id=1, source_target_pairs={{0,15},{1,0},{2,1},{3,2},{4,3},{5,4},{6,5},{7,6},{8,7},{9,8},{10,9... | collective-permute-start | bytes 98312 | tf_op jit(solution)/shard_map/ppermute | solution.py:485
  78.0 16.4 %copy-start = (f32[512,1024]{1,0:T(8,128)S(1)}, f32[512,1024]{1,0:T(8,128)}, u32[]{:S(2)}) copy-start(f32[512,1024]{1,0:T(8,128)} %x_ref.1) | copy-start | bytes 6291460
  82.3 4.6 %collective-permute-start.4 = (f32[8,1024]{1,0:T(8,128)S(1)}, f32[8,1024]{1,0:T(8,128)S(1)}, u32[]{:S(2)}, u32[]{:S(2)}) collective-permute-start(f32[8,1024]{1,0:T(8,128)S(1)} %get-tuple-element.25), channel_id=1, source_target_pairs={{0,16},{16,32},{32,48},{48,64},{64,80},{80,96},{96,112},{112,0},{1... | collective-permute-start | bytes 98312 | tf_op jit(solution)/shard_map/ppermute | solution.py:485
  82.5 4.4 %collective-permute-start.5 = (f32[8,1024]{1,0:T(8,128)S(1)}, f32[8,1024]{1,0:T(8,128)S(1)}, u32[]{:S(2)}, u32[]{:S(2)}) collective-permute-start(f32[8,1024]{1,0:T(8,128)S(1)} %get-tuple-element.26), channel_id=1, source_target_pairs={{0,112},{16,0},{32,16},{48,32},{64,48},{80,64},{96,80},{112,96},{1... | collective-permute-start | bytes 98312 | tf_op jit(solution)/shard_map/ppermute | solution.py:485
  86.9 7.4 %collective-permute-start.6 = (f32[8,1280]{1,0:T(8,128)S(1)}, f32[8,1280]{1,0:T(8,128)S(1)}, u32[]{:S(2)}, u32[]{:S(2)}) collective-permute-start(f32[8,1280]{1,0:T(8,128)S(1)} %get-tuple-element.40), channel_id=1, source_target_pairs={{0,1},{1,2},{2,3},{3,4},{4,5},{5,6},{6,7},{7,8},{8,9},{9,10},{10,1... | collective-permute-start | bytes 122888 | tf_op jit(solution)/shard_map/ppermute | solution.py:485
  87.4 6.9 %collective-permute-start.7 = (f32[8,1280]{1,0:T(8,128)S(1)}, f32[8,1280]{1,0:T(8,128)S(1)}, u32[]{:S(2)}, u32[]{:S(2)}) collective-permute-start(f32[8,1280]{1,0:T(8,128)S(1)} %get-tuple-element.39), channel_id=1, source_target_pairs={{0,15},{1,0},{2,1},{3,2},{4,3},{5,4},{6,5},{7,6},{8,7},{9,8},{10,9... | collective-permute-start | bytes 122888 | tf_op jit(solution)/shard_map/ppermute | solution.py:485

commit v2 on v1

--- a/solution.py
+++ b/solution.py
@@ -13,7 +13,7 @@
 HALO = 8
 LANES = 128
 HAT = 256
-VMEM_LIMIT = 48 << 20
+VMEM_LIMIT = 24 << 20
 PACK_LIMIT = 60 << 20
 
 
@@ -267,17 +267,274 @@
     )(source, rank, incoming, share, weight, hat_x, hat_y)
 
 
-def fill_halo(target, height, width, above, below, left, right, above_side, below_side):
-    tiles = width // LANES
-    first = 2 * HALO
-    end = first + height
+def split(value):
+    high = value.astype(jnp.bfloat16)
+    return high, (value - high.astype(jnp.float32)).astype(jnp.bfloat16)
+
+
+def heun_loops(
+    field, middle, speed, height, chunk, last_chunk, make_across, store_last, after_last
+):
+    count = field.shape[0]
+    scale = TIME_STEP * DIFFUSION / 12.0
+
+    def advance(source, start, size, store):
+        across_of = make_across(source, start, size)
+        for t in range(count):
+            across = across_of(t)
+            one_below = source[t, pl.ds(start - 1, size), :]
+            one_above = source[t, pl.ds(start + 1, size), :]
+            two_below = source[t, pl.ds(start - 2, size), :]
+            two_above = source[t, pl.ds(start + 2, size), :]
+            curve = 16.0 * (one_above + one_below) - (two_above + two_below) + across[:, :LANES]
+            slope = 8.0 * (one_above - one_below) - (two_above - two_below)
+            result = scale * curve - speed[0, t, pl.ds(start, size), :] * slope
+            store(t, result - speed[1, t, pl.ds(start, size), :] * across[:, LANES:])
+
+    def first_half(c, carry):
+        start = pl.multiple_of(HALO + c * chunk, HALO)
+
+        def store(t, result):
+            middle[t, pl.ds(start, chunk), :] = result
+
+        advance(field, start, chunk, store)
+        return carry
+
+    def second_half(c, carry):
+        start = pl.multiple_of(HALO + c * chunk, HALO)
+
+        def store(t, result):
+            field[t, pl.ds(start, chunk), :] = 0.5 * (field[t, pl.ds(start, chunk), :] + result)
+
+        advance(middle, start, chunk, store)
+        return carry
+
+    def last_half(c, carry):
+        start = pl.multiple_of(2 * HALO + c * last_chunk, HALO)
+        place = pl.ds(pl.multiple_of(c * last_chunk, HALO), last_chunk)
+
+        def store(t, result):
+            store_last(t, place, 0.5 * (field[t, pl.ds(start, last_chunk), :] + result))
+
+        advance(middle, start, last_chunk, store)
+        after_last(place)
+        return carry
+
+    extended = (height + 2 * HALO) // chunk
+    for step in range(STEPS):
+        lax.fori_loop(0, extended, first_half, 0)
+        if step < STEPS - 1:
+            lax.fori_loop(0, extended, second_half, 0)
+    lax.fori_loop(0, height // last_chunk, last_half, 0)
+
+
+def largest_chunk(rows, limit):
+    return max(size for size in range(16, limit + 1, 16) if rows % size == 0)
+
+
+def chunks(height):
+    return largest_chunk(height + 2 * HALO, 192), largest_chunk(height, 192)
+
+
+def main_kernel(
+    nodal_ref, speed, stencil_ref, rows_above, rows_below, out_ref, field, middle, result_ref, sem
+):
+    tiles, height, _ = nodal_ref.shape
+    first, end = 2 * HALO, 2 * HALO + height
     for t in range(tiles):
-        target[t, HALO:first, :] = above[:, t * LANES : (t + 1) * LANES]
-        target[t, end : end + HALO, :] = below[:, t * LANES : (t + 1) * LANES]
-    between = jnp.zeros((LANES - 2 * HALO, height), jnp.float32)
-    target[tiles, first:end, :] = jnp.concatenate([right, between, left], axis=0).T
-    target[tiles, HALO:first, :] = above_side
-    target[tiles, end : end + HALO, :] = below_side
+        lanes = slice(t * LANES, (t + 1) * LANES)
+        field[t, first:end, :] = nodal_ref[t]
+        field[t, HALO:first, :] = rows_above[:, lanes]
+        field[t, end : end + HALO, :] = rows_below[:, lanes]
+
+    def make_across(source, start, size):
+        parts = {}
+        lane = lax.broadcasted_iota(jnp.int32, (size, LANES), 1)
+
+        def part(t):
+            if t not in parts:
+                parts[t] = split(source[t, pl.ds(start, size), :])
+            return parts[t]
+
+        def across_of(t):
+            before, after = part((t - 1) % tiles), part((t + 1) % tiles)
+            around = [jnp.where(lane >= LANES // 2, b, a) for b, a in zip(before, after)]
+            return jnp.dot(
+                jnp.concatenate([*part(t), *around], axis=1),
+                stencil_ref[...],
+                preferred_element_type=jnp.float32,
+            )
+
+        return across_of
+
+    def store_last(t, place, value):
+        result_ref[place, t * LANES : (t + 1) * LANES] = value
+
+    def after_last(place):
+        pltpu.make_async_copy(result_ref.at[place], out_ref.at[place], sem).start()
+
+    heun_loops(
+        field, middle, speed, height, *chunks(height), make_across, store_last, after_last
+    )
+    pltpu.make_async_copy(result_ref, out_ref, sem).wait()
+
+
+def main_steps(nodal, speed, stencil, above, below):
+    tiles, height, _ = nodal.shape
+    vmem = pl.BlockSpec(memory_space=pltpu.VMEM)
+    extended = (tiles, height + 4 * HALO, LANES)
+    cells = height * tiles * LANES
+    return pl.pallas_call(
+        main_kernel,
+        out_shape=jax.ShapeDtypeStruct((height, tiles * LANES), jnp.float32),
+        in_specs=[vmem] * 5,
+        out_specs=pl.BlockSpec(memory_space=pl.ANY),
+        scratch_shapes=[
+            pltpu.VMEM(extended, jnp.float32),
+            pltpu.VMEM(extended, jnp.float32),
+            pltpu.VMEM((height, tiles * LANES), jnp.float32),
+            pltpu.SemaphoreType.DMA,
+        ],
+        compiler_params=pltpu.CompilerParams(vmem_limit_bytes=VMEM_LIMIT),
+        cost_estimate=pl.CostEstimate(
+            flops=4 * 2 * cells * 8 * LANES, bytes_accessed=16 * cells, transcendentals=0
+        ),
+        name="heun_main",
+    )(nodal, speed, stencil, above, below)
+
+
+def mix(i, inner, outer):
+    lower = lax.broadcasted_iota(jnp.int32, inner.shape, inner.ndim - 1) < LANES // 2
+    return jnp.where(lower, inner, outer) if i == 0 else jnp.where(lower, outer, inner)
+
+
+def outer_columns(i, columns):
+    rest = jnp.zeros((LANES - HALO, columns.shape[1]), jnp.float32)
+    return jnp.concatenate([rest, columns] if i == 0 else [columns, rest], axis=0).T
+
+
+def spread_kernel(
+    x_ref, y_ref, above_ref, below_ref, left_ref, right_ref, speed_ref, rim_ref
+):
+    height, width = x_ref.shape
+    first, end = 2 * HALO, 2 * HALO + height
+    scale = TIME_STEP / 12.0
+    for f, velocity in enumerate((x_ref, y_ref)):
+        for t in range(width // LANES):
+            lanes = slice(t * LANES, (t + 1) * LANES)
+            speed_ref[f, t, first:end, :] = velocity[:, lanes] * scale
+            speed_ref[f, t, HALO:first, :] = above_ref[f, :, lanes] * scale
+            speed_ref[f, t, end : end + HALO, :] = below_ref[f, :, lanes] * scale
+        for i, received in enumerate((left_ref, right_ref)):
+            lanes = slice(i * (width - LANES), i * (width - LANES) + LANES)
+            outer = outer_columns(i, received[f])
+            rim_ref[f, i, first:end, :] = mix(i, velocity[:, lanes], outer) * scale
+            rim_ref[f, i, HALO:first, :] = above_ref[f, :, lanes] * scale
+            rim_ref[f, i, end : end + HALO, :] = below_ref[f, :, lanes] * scale
+
+
+def spread(x, y, *halo):
+    height, width = x.shape
+    vmem = pl.BlockSpec(memory_space=pltpu.VMEM)
+    rows = height + 4 * HALO
+    return pl.pallas_call(
+        spread_kernel,
+        out_shape=[
+            jax.ShapeDtypeStruct((2, width // LANES, rows, LANES), jnp.float32),
+            jax.ShapeDtypeStruct((2, 2, rows, LANES), jnp.float32),
+        ],
+        in_specs=[vmem] * (2 + len(halo)),
+        out_specs=[vmem, vmem],
+        compiler_params=pltpu.CompilerParams(vmem_limit_bytes=VMEM_LIMIT),
+        cost_estimate=pl.CostEstimate(
+            flops=4 * height * width, bytes_accessed=20 * height * width, transcendentals=0
+        ),
+        name="spread_velocity",
+    )(x, y, *halo)
+
+
+def rim_kernel(
+    main_ref, nodal_ref, rim_ref, stencil_ref, rows_above, rows_below, from_left, from_right, out_ref,
+    field, middle, speed, result_ref, sem,
+):
+    tiles, height, _ = nodal_ref.shape
+    width = tiles * LANES
+    first, end = 2 * HALO, 2 * HALO + height
+    sides = (slice(0, LANES), slice(width - LANES, width))
+    fetches = [
+        pltpu.make_async_copy(main_ref.at[:, pl.ds(side.start, LANES)], result_ref.at[i], sem.at[i])
+        for i, side in enumerate(sides)
+    ]
+    for fetch in fetches:
+        fetch.start()
+
+    def corner(received, k):
+        return received[:, height + k * LANES : height + (k + 1) * LANES]
+
+    for i, (side, received) in enumerate(zip(sides, (from_left, from_right))):
+        field[i, first:end, :] = mix(
+            i, nodal_ref[i * (tiles - 1)], outer_columns(i, received[:, :height])
+        )
+        field[i, HALO:first, :] = mix(i, rows_above[:, side], corner(received, 0))
+        field[i, end : end + HALO, :] = mix(i, rows_below[:, side], corner(received, 1))
+        for f in range(2):
+            speed[f, i, first:end, :] = rim_ref[f, i, first:end, :]
+            for k, rows in enumerate((slice(HALO, first), slice(end, end + HALO))):
+                speed[f, i, rows, :] = mix(
+                    i, rim_ref[f, i, rows, :], corner(received, 2 + 2 * f + k) * (TIME_STEP / 12.0)
+                )
+    for fetch in fetches:
+        fetch.wait()
+
+    def make_across(source, start, size):
+        def across_of(t):
+            return jnp.dot(
+                jnp.concatenate(split(source[t, pl.ds(start, size), :]), axis=1),
+                stencil_ref[...],
+                preferred_element_type=jnp.float32,
+            )
+
+        return across_of
+
+    def store_last(t, place, value):
+        lane = lax.broadcasted_iota(jnp.int32, value.shape, 1)
+        wanted = lane < HALO if t == 0 else lane >= LANES - HALO
+        result_ref[t, place, :] = jnp.where(wanted, value, result_ref[t, place, :])
+
+    heun_loops(
+        field, middle, speed, height, *chunks(height), make_across, store_last, lambda place: None
+    )
+    stores = [
+        pltpu.make_async_copy(result_ref.at[i], out_ref.at[:, pl.ds(side.start, LANES)], sem.at[i])
+        for i, side in enumerate(sides)
+    ]
+    for store in stores:
+        store.start()
+    for store in stores:
+        store.wait()
+
+
+def rim_steps(main, nodal, speed, stencil, *halo):
+    _, height, _ = nodal.shape
+    vmem = pl.BlockSpec(memory_space=pltpu.VMEM)
+    anywhere = pl.BlockSpec(memory_space=pl.ANY)
+    extended = (2, height + 4 * HALO, LANES)
+    return pl.pallas_call(
+        rim_kernel,
+        out_shape=jax.ShapeDtypeStruct(main.shape, jnp.float32),
+        in_specs=[anywhere] + [vmem] * (3 + len(halo)),
+        out_specs=anywhere,
+        input_output_aliases={0: 0},
+        scratch_shapes=[
+            pltpu.VMEM(extended, jnp.float32),
+            pltpu.VMEM(extended, jnp.float32),
+            pltpu.VMEM((2,) + extended, jnp.float32),
+            pltpu.VMEM((2, height, LANES), jnp.float32),
+            pltpu.SemaphoreType.DMA((2,)),
+        ],
+        compiler_params=pltpu.CompilerParams(vmem_limit_bytes=VMEM_LIMIT),
+        name="heun_rim",
+    )(main, nodal, speed, stencil, *halo)
 
 
 def edges_kernel(*refs):
@@ -309,140 +566,7 @@
     )(*[x] * 4, *[y] * 4)
 
 
-def steps_kernel(
-    chunk, last_chunk, nodal_ref, x_ref, y_ref, stencil_ref, rows_above, rows_below, speed_above,
-    speed_below, speed_left, speed_right, from_left, from_right, out_ref, field, middle, speed, result_ref, sem,
-):
-    tiles, height, _ = nodal_ref.shape
-    width = tiles * LANES
-    count = tiles + 1
-    scale = TIME_STEP * DIFFUSION / 12.0
-    speed_scale = TIME_STEP / 12.0
-    side = lax.broadcasted_iota(jnp.int32, (HALO, LANES), 1)
-
-    def corner(k):
-        part = slice(height + k * LANES, height + (k + 1) * LANES)
-        return jnp.where(side < LANES // 2, from_right[:, part], from_left[:, part])
-
-    for t in range(tiles):
-        field[t, 2 * HALO : 2 * HALO + height, :] = nodal_ref[t]
-    fill_halo(
-        field, height, width, rows_above, rows_below, from_left[:, :height], from_right[:, :height],
-        corner(0), corner(1),
-    )
-    for f, velocity in enumerate((x_ref, y_ref)):
-        for t in range(tiles):
-            speed[f, t, 2 * HALO : 2 * HALO + height, :] = (
-                velocity[:, t * LANES : (t + 1) * LANES] * speed_scale
-            )
-        fill_halo(
-            speed.at[f], height, width, speed_above[f] * speed_scale, speed_below[f] * speed_scale,
-            speed_left[f] * speed_scale, speed_right[f] * speed_scale,
-            corner(2 + 2 * f) * speed_scale, corner(3 + 2 * f) * speed_scale,
-        )
-
-    def advance(source, start, size, tile_range, store):
-        parts = {}
-        lane = lax.broadcasted_iota(jnp.int32, (size, LANES), 1)
-
-        def split(t):
-            if t not in parts:
-                value = source[t, pl.ds(start, size), :]
-                high = value.astype(jnp.bfloat16)
-                parts[t] = (high, (value - high.astype(jnp.float32)).astype(jnp.bfloat16))
-            return parts[t]
-
-        for t in tile_range:
-            before, after = split((t - 1) % count), split((t + 1) % count)
-            around = [jnp.where(lane >= LANES // 2, b, a) for b, a in zip(before, after)]
-            across = jnp.dot(
-                jnp.concatenate([*split(t), *around], axis=1),
-                stencil_ref[...],
-                preferred_element_type=jnp.float32,
-            )
-            one_below = source[t, pl.ds(start - 1, size), :]
-            one_above = source[t, pl.ds(start + 1, size), :]
-            two_below = source[t, pl.ds(start - 2, size), :]
-            two_above = source[t, pl.ds(start + 2, size), :]
-            curve = 16.0 * (one_above + one_below) - (two_above + two_below) + across[:, :LANES]
-            slope = 8.0 * (one_above - one_below) - (two_above - two_below)
-            result = scale * curve - speed[0, t, pl.ds(start, size), :] * slope
-            store(t, result - speed[1, t, pl.ds(start, size), :] * across[:, LANES:])
-
-    def first_half(c, carry):
-        start = pl.multiple_of(HALO + c * chunk, HALO)
-
-        def store(t, result):
-            middle[t, pl.ds(start, chunk), :] = result
-
-        advance(field, start, chunk, range(count), store)
-        return carry
-
-    def second_half(c, carry):
-        start = pl.multiple_of(HALO + c * chunk, HALO)
-
-        def store(t, result):
-            field[t, pl.ds(start, chunk), :] = 0.5 * (field[t, pl.ds(start, chunk), :] + result)
-
-        advance(middle, start, chunk, range(count), store)
-        return carry
-
-    def last_half(c, carry):
-        start = pl.multiple_of(2 * HALO + c * last_chunk, HALO)
-        place = pl.multiple_of(c * last_chunk, HALO)
-
-        def store(t, result):
-            result_ref[pl.ds(place, last_chunk), t * LANES : (t + 1) * LANES] = 0.5 * (
-                field[t, pl.ds(start, last_chunk), :] + result
-            )
-
-        advance(middle, start, last_chunk, range(tiles), store)
-        rows = pl.ds(place, last_chunk)
-        pltpu.make_async_copy(result_ref.at[rows], out_ref.at[rows], sem).start()
-        return carry
-
-    extended = (height + 2 * HALO) // chunk
-    for step in range(STEPS):
-        lax.fori_loop(0, extended, first_half, 0)
-        if step < STEPS - 1:
-            lax.fori_loop(0, extended, second_half, 0)
-    lax.fori_loop(0, height // last_chunk, last_half, 0)
-    pltpu.make_async_copy(result_ref, out_ref, sem).wait()
-
-
-def largest_chunk(rows, limit):
-    return max(size for size in range(16, limit + 1, 16) if rows % size == 0)
-
-
-def run_steps(nodal, x, y, stencil, *halo):
-    tiles, height, _ = nodal.shape
-    vmem = pl.BlockSpec(memory_space=pltpu.VMEM)
-    extended = (tiles + 1, height + 4 * HALO, LANES)
-    return pl.pallas_call(
-        functools.partial(
-            steps_kernel, largest_chunk(height + 2 * HALO, 192), largest_chunk(height, 192)
-        ),
-        out_shape=jax.ShapeDtypeStruct((height, tiles * LANES), jnp.float32),
-        in_specs=[vmem] * (4 + len(halo)),
-        out_specs=pl.BlockSpec(memory_space=pl.ANY),
-        scratch_shapes=[
-            pltpu.VMEM(extended, jnp.float32),
-            pltpu.VMEM(extended, jnp.float32),
-            pltpu.VMEM((2,) + extended, jnp.float32),
-            pltpu.VMEM((height, tiles * LANES), jnp.float32),
-            pltpu.SemaphoreType.DMA,
-        ],
-        compiler_params=pltpu.CompilerParams(vmem_limit_bytes=VMEM_LIMIT),
-        name="heun_steps",
-    )(nodal, x, y, stencil, *halo)
-
-
-def stencil_matrix():
-    row = lax.broadcasted_iota(jnp.int32, (4 * LANES, 2 * LANES), 0)
-    column = lax.broadcasted_iota(jnp.int32, (4 * LANES, 2 * LANES), 1)
-    lane = row % LANES
-    outside = jnp.where(lane < LANES // 2, lane + LANES, lane - LANES)
-    shift = jnp.where(row < 2 * LANES, lane, outside) - column % LANES
+def stencil_entries(shift, column):
     distance = jnp.abs(shift)
     centre = 12.0 / (TIME_STEP * DIFFUSION) - 60.0
     curve = jnp.where(distance == 1, 16.0, jnp.where(distance == 2, -1.0, 0.0))
@@ -451,6 +575,17 @@
         shift
     ).astype(jnp.float32)
     return jnp.where(column < LANES, curve, slope).astype(jnp.bfloat16)
+
+
+def stencil_matrices():
+    row = lax.broadcasted_iota(jnp.int32, (4 * LANES, 2 * LANES), 0)
+    column = lax.broadcasted_iota(jnp.int32, (4 * LANES, 2 * LANES), 1)
+    lane = row % LANES
+    outside = jnp.where(lane < LANES // 2, lane + LANES, lane - LANES)
+    shift = jnp.where(row < 2 * LANES, lane, outside) - column % LANES
+    ring = lane - column % LANES
+    ring = jnp.where(ring > LANES // 2, ring - LANES, jnp.where(ring < -LANES // 2, ring + LANES, ring))
+    return stencil_entries(shift, column), stencil_entries(ring, column)[: 2 * LANES]
 
 
 def hat_matrix(size):
@@ -480,9 +615,14 @@
     return jnp.sum(jnp.where(covered, share[:, None, None], 0.0), axis=0)
 
 
-def shifted(array, axis, by):
+def exchange(first, last, axis):
     size = lax.axis_size(axis)
-    return lax.ppermute(array, axis, [(i, (i + by) % size) for i in range(size)])
+    even = lax.axis_index(axis) % 2 == 0
+    inner = [(i, i ^ 1) for i in range(size)]
+    outer = [((i + 1) % size, ((i ^ 1) + 1) % size) for i in range(size)]
+    by_inner = lax.ppermute(jnp.where(even, last, first), axis, inner)
+    by_outer = lax.ppermute(jnp.where(even, first, last), axis, outer)
+    return jnp.where(even, by_outer, by_inner), jnp.where(even, by_inner, by_outer)
 
 
 def lead_share(offsets, index_x, index_y, size_x, size_y, tiles_across, tile_height):
@@ -533,10 +673,8 @@
 
     first_rows, last_rows, first_cols, last_cols = edges(velocity_x, velocity_y)
     speed_halo = (
-        shifted(last_rows, "gx", 1),
-        shifted(first_rows, "gx", -1),
-        shifted(last_cols, "gy", 1),
-        shifted(first_cols, "gy", -1),
+        *exchange(first_rows, last_rows, "gx"),
+        *exchange(first_cols, last_cols, "gy"),
     )
     incoming, speed_halo = lax.optimization_barrier((incoming, speed_halo))
     share = lead_share(offsets, index_x, index_y, size_x, size_y, tiles_across, tile_height)
@@ -547,18 +685,18 @@
         source, slot_rank, incoming, share, weight, hat, hat.T, rows_local, cols_local, tile_height,
         capacity,
     )
-    above = shifted(last_rows, "gx", 1)
-    below = shifted(first_rows, "gx", -1)
+    speed_halo, nodal = lax.optimization_barrier((speed_halo, nodal))
+    speed, rim_speed = spread(velocity_x, velocity_y, *speed_halo)
+    above, below = exchange(first_rows, last_rows, "gx")
     strips = [above, below] + [side[f] for f in range(2) for side in speed_halo[:2]]
-    from_left = shifted(
-        jnp.concatenate([last_cols] + [strip[:, -LANES:] for strip in strips], axis=1), "gy", 1
-    )
-    from_right = shifted(
-        jnp.concatenate([first_cols] + [strip[:, :LANES] for strip in strips], axis=1), "gy", -1
-    )
-    return run_steps(
-        nodal, velocity_x, velocity_y, stencil_matrix(), above, below, *speed_halo, from_left, from_right
-    )
+    from_left, from_right = exchange(
+        jnp.concatenate([first_cols] + [strip[:, :LANES] for strip in strips], axis=1),
+        jnp.concatenate([last_cols] + [strip[:, -LANES:] for strip in strips], axis=1),
+        "gy",
+    )
+    stencil, ring_stencil = stencil_matrices()
+    main = main_steps(nodal, speed, stencil, above, below)
+    return rim_steps(main, nodal, rim_speed, ring_stencil, above, below, from_left, from_right)
 
 
 def solution(mesh):

time: 107 us -> 105 us (0.981)
  waiting for transfers between devices: 48.6 us -> 44.1 us
  Pallas kernels: 21.7 us -> 24.5 us
  starting transfers between devices: 28.3 us -> 25.8 us
  other arithmetic: 5.43 us -> 7.61 us
    ppermute x8, waiting for transfers between devices: 48.1 us -> 43.6 us  [the longest x4 41.2 us: exchange(): by_inner = lax.ppermute(jnp.where(even, last, first), axis, inner)]
    ppermute x8, starting transfers between devices: 16.7 us -> 14.2 us  [the longest x4 11.5 us: exchange(): by_outer = lax.ppermute(jnp.where(even, first, last), axis, outer)]
    pallas_call x1 -> x3, Pallas kernels: 11.8 us -> 14.2 us  [the longest x1 8.84 us: main_steps(): pl.pallas_call(main_kernel, out_shape=jax.ShapeDtypeStruct((height, tiles...]
    select_n x0 -> x8, other arithmetic: none -> 1.72 us  [the longest x4 1.68 us: exchange(): by_inner = lax.ppermute(jnp.where(even, last, first), axis, inner)]
  transfers between devices with their start and end apart: 9 -> 9, of which waited for: 4 -> 4; matrix products, arithmetic and copies ran while one was open for 7% -> 9% of each run, Pallas kernels for 2% -> 11%
where the time goes in v2:
time: 105 us; the launch traced here: 104 us
  waiting for transfers between devices  44.1 us (42%)
  starting transfers between devices  25.8 us (25%)
  Pallas kernels  24.5 us (23%)
  other arithmetic  7.61 us (7%)
  local copies, waits for them, and re-layouts  1.84 us (2%)
    ppermute x4, waiting for transfers between devices, exchange(): by_inner = lax.ppermute(jnp.where(even, last, first), axis, inner)  41.2 us
    all_to_all x1, starting transfers between devices, local(): lax.all_to_all(outgoing, ('gx', 'gy'), split_axis=0, concat_axis=0, tiled...  11.6 us
    ppermute x4, starting transfers between devices, exchange(): by_outer = lax.ppermute(jnp.where(even, first, last), axis, outer)  11.5 us
    pallas_call x1, Pallas kernels, main_steps(): pl.pallas_call(main_kernel, out_shape=jax.ShapeDtypeStruct((height, tiles...  8.84 us
    pallas_call x1, Pallas kernels, refine_block(): pl.pallas_call(functools.partial(refine_kernel, width // HAT, tile_rows,...  4.79 us
    pallas_call x1, Pallas kernels, rim_steps(): pl.pallas_call(rim_kernel, out_shape=jax.ShapeDtypeStruct(main.shape, jnp...  4.67 us
    select_n x1, other arithmetic, lead_share(): jnp.where(line < row_parts, rows, jnp.where(corner < 0, cols, corners))  3.95 us
    pallas_call x1, Pallas kernels, pack(): pl.pallas_call(functools.partial(pack_kernel, tiles_across, capacity), ou...  3.21 us
  transfers between devices with their start and end apart: 9, of which 4 were waited for; matrix products, arithmetic and copies ran while one was open for 9% of the time, Pallas kernels for 11%

profile of v2, /device:TPU:0, one launch (start us, length us, event | category | flops | bytes accessed | tf_op | source)
XLA Modules:
  0.0 104.4 jit_solution(17697291486551055848)
XLA Ops:
  0.0 3.2 %pack_tiles.1 = f32[128,80,128]{2,1,0:T(8,128)} custom-call(s32[16384]{0:T(1024)} %owner_ref.1, f32[128,16,256]{2,1,0:T(8,128)} %owned_ref.1), custom_call_target="tpu_custom_call" | custom-call | tf_op jit(solution)/shard_map/pack_tiles/pallas_call | solution.py:92
  3.2 11.6 %all-to-all-start = ((f32[128,80,128]{2,1,0:T(8,128)}), f32[128,80,128]{2,1,0:T(8,128)}, u32[]{:S(2)}, u32[]{:S(2)}) async-start(f32[128,80,128]{2,1,0:T(8,128)} %pack_tiles.1), calls=%async_computation | async-start | bytes 10485760 | tf_op jit(solution)/shard_map/all_to_all | solution.py:672
  14.9 0.0 copy-start.2
  14.9 0.0 slice-start
  14.9 0.0 copy-start.4
  14.9 0.0 copy-start.5
  14.9 0.0 copy-start.3
  14.9 2.3 %velocity_edges.1 = (f32[2,8,1024]{2,1,0:T(8,128)}, f32[2,8,1024]{2,1,0:T(8,128)}, f32[2,8,512]{2,1,0:T(8,128)}, f32[2,8,512]{2,1,0:T(8,128)}) custom-call(f32[512,1024]{1,0:T(8,128)} %x_ref.1, f32[512,1024]{1,0:T(8,128)} %x_ref.1, f32[512,1024]{1,0:T(8,128)} %x_ref.1, f32[512,1024]{1,0:T(8,128)} %x_ref.1, f32[512,1024]{1,0:T(8,128)} %y_ref.1, ...), custom_call_target="tpu_custom_call" | custom-call | tf_op jit(solution)/shard_map/velocity_edges/pallas_call | solution.py:559
  17.2 0.9 broadcast_select_fusion.2
  18.1 0.1 collective-permute-start.1
  18.2 2.3 %collective-permute-start = (f32[2,8,1024]{2,1,0:T(8,128)S(1)}, f32[2,8,1024]{2,1,0:T(8,128)S(1)}, u32[]{:S(2)}, u32[]{:S(2)}) collective-permute-start(f32[2,8,1024]{2,1,0:T(8,128)S(1)} %get-tuple-element.50), channel_id=1, source_target_pairs={{16,32},{32,16},{48,64},{64,48},{80,96},{96,80},{112,0},{0,112},{1... | collective-permute-start | bytes 196616 | tf_op jit(solution)/shard_map/ppermute | solution.py:624
  20.4 0.8 broadcast_select_fusion.14
  21.2 1.7 %collective-permute-start.3 = (f32[2,8,512]{2,1,0:T(8,128)S(1)}, f32[2,8,512]{2,1,0:T(8,128)S(1)}, u32[]{:S(2)}, u32[]{:S(2)}) collective-permute-start(f32[2,8,512]{2,1,0:T(8,128)S(1)} %get-tuple-element.67), channel_id=1, source_target_pairs={{0,1},{1,0},{2,3},{3,2},{4,5},{5,4},{6,7},{7,6},{8,9},{9,8},{10,11... | collective-permute-start | bytes 98312 | tf_op jit(solution)/shard_map/ppermute | solution.py:623
  22.9 4.5 %collective-permute-start.2 = (f32[2,8,512]{2,1,0:T(8,128)S(1)}, f32[2,8,512]{2,1,0:T(8,128)S(1)}, u32[]{:S(2)}, u32[]{:S(2)}) collective-permute-start(f32[2,8,512]{2,1,0:T(8,128)S(1)} %get-tuple-element.68), channel_id=1, source_target_pairs={{1,2},{2,1},{3,4},{4,3},{5,6},{6,5},{7,8},{8,7},{9,10},{10,9},{11,... | collective-permute-start | bytes 98312 | tf_op jit(solution)/shard_map/ppermute | solution.py:624
  27.4 0.5 slice.74
  27.9 0.1 slice.73
  28.1 0.1 broadcast_in_dim.118
  28.2 0.1 broadcast_in_dim.119
  28.2 0.1 broadcast_in_dim.120
  28.3 0.7 broadcast_in_dim.121
  29.0 0.1 pad.4.clone
  29.1 0.1 broadcast_in_dim.115
  29.1 0.1 reshape.387
  29.3 0.1 compare_reduce_fusion
  29.5 0.1 select_reduce_fusion.weight_ref
  29.6 0.1 add_add_fusion
  29.6 4.0 %select_select_fusion.2 = (f32[1,128,16,128]{3,2,1,0:T(8,128)S(1)}, f32[1,128,16,128]{3,2,1,0:T(8,128)S(1)}) fusion(s32[16]{0:T(128)S(1)} %get-tuple-element.89, s32[16]{0:T(128)S(1)} %get-tuple-element.90, s32[]{:T(128)S(6)} %axis_index.15, s32[]{:T(128)S(6)} %axis_index.17, s32[16,128]{1,0:T(8,128)S(1)} %add_add_fusion, ...), kind=kLoop, calls=%fused_computation.23 | loop fusion | flops 24641536 | bytes 2105520 | tf_op jit(solution)/shard_map/jit(_where)/select_n | solution.py:647
  33.6 0.1 pad_maximum_fusion.share_ref
  33.7 0.2 select_convert_fusion
  33.9 0.7 fusion.14.stencil_ref
  34.6 0.3 fusion.24
  34.9 0.1 fusion.20.stencil_ref
  35.1 0.2 convert_reduce_fusion.rank_ref
  35.2 41.2 %collective-permute-done.3 = f32[2,8,512]{2,1,0:T(8,128)S(1)} collective-permute-done((f32[2,8,512]{2,1,0:T(8,128)S(1)}, f32[2,8,512]{2,1,0:T(8,128)S(1)}, u32[]{:S(2)}, u32[]{:S(2)}) %collective-permute-start.3) | collective-permute-done | bytes 32800 | tf_op jit(solution)/shard_map/ppermute | solution.py:623
  76.4 1.0 collective-permute-done.2
  77.4 0.0 collective-permute-done.1
  77.4 0.0 collective-permute-done
  77.4 0.5 all-to-all-done.incoming_ref
  77.9 4.8 %refine_block.1 = (f32[8,512,128]{2,1,0:T(8,128)S(1)}, f32[8,1024]{1,0:T(8,128)S(1)}, f32[8,1024]{1,0:T(8,128)S(1)}, f32[8,512]{1,0:T(8,128)S(1)}, f32[8,512]{1,0:T(8,128)S(1)}) custom-call(s32[128]{0:T(128)S(1)} %get-tuple-element.64.source_ref, s32[128]{0:T(128)S(1)} %convert_reduce_fusion.rank_ref, f32[128,80,128]{2,1,0:T(8,128)} %all-to-all-done.incoming_ref, ...), custom_call_target="tpu_custom_call" | custom-call | tf_op jit(solution)/shard_map/refine_block/pallas_call | solution.py:252
  82.7 0.3 collective-permute-start.5
  82.9 2.3 %collective-permute-start.4 = (f32[8,1024]{1,0:T(8,128)S(1)}, f32[8,1024]{1,0:T(8,128)S(1)}, u32[]{:S(2)}, u32[]{:S(2)}) collective-permute-start(f32[8,1024]{1,0:T(8,128)S(1)} %get-tuple-element.62), channel_id=1, source_target_pairs={{16,32},{32,16},{48,64},{64,48},{80,96},{96,80},{112,0},{0,112},{1... | collective-permute-start | bytes 98312 | tf_op jit(solution)/shard_map/ppermute | solution.py:624
  85.3 0.7 spread_velocity.1
  86.0 0.0 collective-permute-done.5
  86.0 1.5 %collective-permute-done.4 = f32[8,1024]{1,0:T(8,128)S(1)} collective-permute-done((f32[8,1024]{1,0:T(8,128)S(1)}, f32[8,1024]{1,0:T(8,128)S(1)}, u32[]{:S(2)}, u32[]{:S(2)}) %collective-permute-start.4) | collective-permute-done | bytes 32800 | tf_op jit(solution)/shard_map/ppermute | solution.py:624
  87.6 0.6 collective-permute-start.7
  88.2 2.5 %collective-permute-start.6 = (f32[8,1280]{1,0:T(8,128)S(1)}, f32[8,1280]{1,0:T(8,128)S(1)}, u32[]{:S(2)}, u32[]{:S(2)}) collective-permute-start(f32[8,1280]{1,0:T(8,128)S(1)} %get-tuple-element.54), channel_id=1, source_target_pairs={{1,2},{2,1},{3,4},{4,3},{5,6},{6,5},{7,8},{8,7},{9,10},{10,9},{11,... | collective-permute-start | bytes 122888 | tf_op jit(solution)/shard_map/ppermute | solution.py:624
  90.7 8.8 %heun_main.1.main_ref = f32[512,1024]{1,0:T(8,128)} custom-call(f32[8,512,128]{2,1,0:T(8,128)S(1)} %get-tuple-element.36.nodal_ref, f32[2,8,544,128]{3,2,1,0:T(8,128)S(1)} %get-tuple-element.41.speed, bf16[512,256]{1,0:T(8,128)(2,1)S(1)} %fusion.14.stencil_ref, f32[8,1024]{1,0:T(8,128)S(1)} %get-tuple-element.60.rows_above, ...), custom_call_target="tpu_custom_call" | custom-call | flops 4294967296 | bytes 8388608 | tf_op jit(solution)/shard_map/heun_main/pallas_call | solution.py:387
  99.6 4.7 %heun_rim.1 = f32[512,1024]{1,0:T(8,128)} custom-call(f32[512,1024]{1,0:T(8,128)} %heun_main.1.main_ref, f32[8,512,128]{2,1,0:T(8,128)S(1)} %get-tuple-element.36.nodal_ref, f32[2,2,544,128]{3,2,1,0:T(8,128)S(1)} %get-tuple-element.44.rim_ref, bf16[256,256]{1,0:T(8,128)(2,1)S(1)} %fusion.20.stencil_ref, ...), custom_call_target="tpu_custom_call", output_to_operand_aliasing={{}: (0, {})} | custom-call | tf_op jit(solution)/shard_map/heun_rim/pallas_call | solution.py:522
  (41 shorter events, 0.2 us)
Async XLA Ops:
  3.2 74.6 %all-to-all-start = ((f32[128,80,128]{2,1,0:T(8,128)}), f32[128,80,128]{2,1,0:T(8,128)}, u32[]{:S(2)}, u32[]{:S(2)}) async-start(f32[128,80,128]{2,1,0:T(8,128)} %pack_tiles.1), calls=%async_computation | async-start | bytes 10485760 | tf_op jit(solution)/shard_map/all_to_all | solution.py:672
  14.9 12.6 %copy-start.2 = (s32[16384]{0:T(1024)S(1)}, s32[16384]{0:T(1024)}, u32[]{:S(2)}) copy-start(s32[16384]{0:T(1024)} %owner_ref.1) | copy-start | bytes 196612
  14.9 14.2 %slice-start = ((s32[16384]{0:T(1024)}), s32[4]{0:T(128)S(1)}, s32[]{:S(2)}) async-start(s32[16384]{0:T(1024)} %owner_ref.1), calls=%async_computation.1 | async-start | bytes 1024 | tf_op jit(solution)/shard_map/slice | solution.py:631
  14.9 14.5 %copy-start.4 = (s32[2]{0:T(128)S(1)}, s32[2]{0:T(128)}, u32[]{:S(2)}) copy-start(s32[2]{0:T(128)} %param.11) | copy-start | bytes 28
  14.9 14.5 %copy-start.5 = (s32[8]{0:T(128)S(1)}, s32[8]{0:T(128)}, u32[]{:S(2)}) copy-start(s32[8]{0:T(128)} %param.10) | copy-start | bytes 100
  14.9 14.5 %copy-start.3 = (s32[8,2]{0,1:T(2,128)S(1)}, s32[8,2]{0,1:T(2,128)}, u32[]{:S(2)}) copy-start(s32[8,2]{0,1:T(2,128)} %param.9) | copy-start | bytes 196
  18.1 59.3 %collective-permute-start.1 = (f32[2,8,1024]{2,1,0:T(8,128)S(1)}, f32[2,8,1024]{2,1,0:T(8,128)S(1)}, u32[]{:S(2)}, u32[]{:S(2)}) collective-permute-start(f32[2,8,1024]{2,1,0:T(8,128)S(1)} %get-tuple-element.49), channel_id=1, source_target_pairs={{0,16},{16,0},{32,48},{48,32},{64,80},{80,64},{96,112},{112,96},{1... | collective-permute-start | bytes 196616 | tf_op jit(solution)/shard_map/ppermute | solution.py:623
  18.2 59.2 %collective-permute-start = (f32[2,8,1024]{2,1,0:T(8,128)S(1)}, f32[2,8,1024]{2,1,0:T(8,128)S(1)}, u32[]{:S(2)}, u32[]{:S(2)}) collective-permute-start(f32[2,8,1024]{2,1,0:T(8,128)S(1)} %get-tuple-element.50), channel_id=1, source_target_pairs={{16,32},{32,16},{48,64},{64,48},{80,96},{96,80},{112,0},{0,112},{1... | collective-permute-start | bytes 196616 | tf_op jit(solution)/shard_map/ppermute | solution.py:624
  21.2 55.2 %collective-permute-start.3 = (f32[2,8,512]{2,1,0:T(8,128)S(1)}, f32[2,8,512]{2,1,0:T(8,128)S(1)}, u32[]{:S(2)}, u32[]{:S(2)}) collective-permute-start(f32[2,8,512]{2,1,0:T(8,128)S(1)} %get-tuple-element.67), channel_id=1, source_target_pairs={{0,1},{1,0},{2,3},{3,2},{4,5},{5,4},{6,7},{7,6},{8,9},{9,8},{10,11... | collective-permute-start | bytes 98312 | tf_op jit(solution)/shard_map/ppermute | solution.py:623
  22.9 54.4 %collective-permute-start.2 = (f32[2,8,512]{2,1,0:T(8,128)S(1)}, f32[2,8,512]{2,1,0:T(8,128)S(1)}, u32[]{:S(2)}, u32[]{:S(2)}) collective-permute-start(f32[2,8,512]{2,1,0:T(8,128)S(1)} %get-tuple-element.68), channel_id=1, source_target_pairs={{1,2},{2,1},{3,4},{4,3},{5,6},{6,5},{7,8},{8,7},{9,10},{10,9},{11,... | collective-permute-start | bytes 98312 | tf_op jit(solution)/shard_map/ppermute | solution.py:624
  77.9 7.4 %copy-start = (f32[512,1024]{1,0:T(8,128)S(1)}, f32[512,1024]{1,0:T(8,128)}, u32[]{:S(2)}) copy-start(f32[512,1024]{1,0:T(8,128)} %x_ref.1) | copy-start | bytes 6291460
  77.9 7.4 %copy-start.1 = (f32[512,1024]{1,0:T(8,128)S(1)}, f32[512,1024]{1,0:T(8,128)}, u32[]{:S(2)}) copy-start(f32[512,1024]{1,0:T(8,128)} %y_ref.1) | copy-start | bytes 6291460
  82.7 3.3 %collective-permute-start.5 = (f32[8,1024]{1,0:T(8,128)S(1)}, f32[8,1024]{1,0:T(8,128)S(1)}, u32[]{:S(2)}, u32[]{:S(2)}) collective-permute-start(f32[8,1024]{1,0:T(8,128)S(1)} %get-tuple-element.61), channel_id=1, source_target_pairs={{0,16},{16,0},{32,48},{48,32},{64,80},{80,64},{96,112},{112,96},{1... | collective-permute-start | bytes 98312 | tf_op jit(solution)/shard_map/ppermute | solution.py:623
  82.9 4.6 %collective-permute-start.4 = (f32[8,1024]{1,0:T(8,128)S(1)}, f32[8,1024]{1,0:T(8,128)S(1)}, u32[]{:S(2)}, u32[]{:S(2)}) collective-permute-start(f32[8,1024]{1,0:T(8,128)S(1)} %get-tuple-element.62), channel_id=1, source_target_pairs={{16,32},{32,16},{48,64},{64,48},{80,96},{96,80},{112,0},{0,112},{1... | collective-permute-start | bytes 98312 | tf_op jit(solution)/shard_map/ppermute | solution.py:624
  87.6 11.9 %collective-permute-start.7 = (f32[8,1280]{1,0:T(8,128)S(1)}, f32[8,1280]{1,0:T(8,128)S(1)}, u32[]{:S(2)}, u32[]{:S(2)}) collective-permute-start(f32[8,1280]{1,0:T(8,128)S(1)} %get-tuple-element.53), channel_id=1, source_target_pairs={{0,1},{1,0},{2,3},{3,2},{4,5},{5,4},{6,7},{7,6},{8,9},{9,8},{10,11... | collective-permute-start | bytes 122888 | tf_op jit(solution)/shard_map/ppermute | solution.py:623
  88.2 11.3 %collective-permute-start.6 = (f32[8,1280]{1,0:T(8,128)S(1)}, f32[8,1280]{1,0:T(8,128)S(1)}, u32[]{:S(2)}, u32[]{:S(2)}) collective-permute-start(f32[8,1280]{1,0:T(8,128)S(1)} %get-tuple-element.54), channel_id=1, source_target_pairs={{1,2},{2,1},{3,4},{4,3},{5,6},{6,5},{7,8},{8,7},{9,10},{10,9},{11,... | collective-permute-start | bytes 122888 | tf_op jit(solution)/shard_map/ppermute | solution.py:624

commit v3 on v2

--- a/solution.py
+++ b/solution.py
@@ -15,6 +15,7 @@
 HAT = 256
 VMEM_LIMIT = 24 << 20
 PACK_LIMIT = 60 << 20
+REFINE_LIMIT = 40 << 20
 
 
 def pack_kernel(
@@ -116,11 +117,9 @@
     value = left if split_left else right
     high = value.astype(jnp.bfloat16)
     low = (value - high.astype(jnp.float32)).astype(jnp.bfloat16)
-    if split_left:
-        pairs = ((high, right), (low, right))
-    else:
-        pairs = ((left, high), (left, low))
-    return sum(jnp.dot(a, b, preferred_element_type=jnp.float32) for a, b in pairs)
+    both = jnp.concatenate([high, low], axis=1 if split_left else 0)
+    pair = (both, right) if split_left else (left, both)
+    return jnp.dot(*pair, preferred_element_type=jnp.float32)
 
 
 def refine_kernel(
@@ -262,7 +261,7 @@
             pltpu.SemaphoreType.DMA((4,)),
             pltpu.SemaphoreType.DMA,
         ],
-        compiler_params=pltpu.CompilerParams(vmem_limit_bytes=VMEM_LIMIT),
+        compiler_params=pltpu.CompilerParams(vmem_limit_bytes=REFINE_LIMIT),
         name="refine_block",
     )(source, rank, incoming, share, weight, hat_x, hat_y)
 
@@ -332,8 +331,8 @@
     return max(size for size in range(16, limit + 1, 16) if rows % size == 0)
 
 
-def chunks(height):
-    return largest_chunk(height + 2 * HALO, 192), largest_chunk(height, 192)
+def chunks(height, limit):
+    return largest_chunk(height + 2 * HALO, limit), largest_chunk(height, limit)
 
 
 def main_kernel(
@@ -356,16 +355,17 @@
                 parts[t] = split(source[t, pl.ds(start, size), :])
             return parts[t]
 
-        def across_of(t):
+        def inputs(t):
             before, after = part((t - 1) % tiles), part((t + 1) % tiles)
             around = [jnp.where(lane >= LANES // 2, b, a) for b, a in zip(before, after)]
-            return jnp.dot(
-                jnp.concatenate([*part(t), *around], axis=1),
-                stencil_ref[...],
-                preferred_element_type=jnp.float32,
-            )
-
-        return across_of
+            return jnp.concatenate([*part(t), *around], axis=1)
+
+        across = jnp.dot(
+            jnp.concatenate([inputs(t) for t in range(tiles)], axis=0),
+            stencil_ref[...],
+            preferred_element_type=jnp.float32,
+        )
+        return lambda t: across[t * size : (t + 1) * size]
 
     def store_last(t, place, value):
         result_ref[place, t * LANES : (t + 1) * LANES] = value
@@ -374,7 +374,7 @@
         pltpu.make_async_copy(result_ref.at[place], out_ref.at[place], sem).start()
 
     heun_loops(
-        field, middle, speed, height, *chunks(height), make_across, store_last, after_last
+        field, middle, speed, height, *chunks(height, 192), make_across, store_last, after_last
     )
     pltpu.make_async_copy(result_ref, out_ref, sem).wait()
 
@@ -403,14 +403,17 @@
     )(nodal, speed, stencil, above, below)
 
 
-def mix(i, inner, outer):
-    lower = lax.broadcasted_iota(jnp.int32, inner.shape, inner.ndim - 1) < LANES // 2
-    return jnp.where(lower, inner, outer) if i == 0 else jnp.where(lower, outer, inner)
-
-
-def outer_columns(i, columns):
-    rest = jnp.zeros((LANES - HALO, columns.shape[1]), jnp.float32)
-    return jnp.concatenate([rest, columns] if i == 0 else [columns, rest], axis=0).T
+def quarters(first, last, after, before):
+    quarter = lax.broadcasted_iota(jnp.int32, first.shape, 1) // (LANES // 4)
+    inner = jnp.where(quarter == 0, first, pltpu.roll(last, LANES // 2, axis=1))
+    return jnp.where(quarter < 2, inner, jnp.where(quarter == 2, after, before))
+
+
+def outer_columns(before, after):
+    height = before.shape[1]
+    low = jnp.zeros((LANES // 2, height), jnp.float32)
+    high = jnp.zeros((LANES // 2 - 2 * HALO, height), jnp.float32)
+    return jnp.concatenate([low, after, high, before], axis=0).T
 
 
 def spread_kernel(
@@ -425,12 +428,12 @@
             speed_ref[f, t, first:end, :] = velocity[:, lanes] * scale
             speed_ref[f, t, HALO:first, :] = above_ref[f, :, lanes] * scale
             speed_ref[f, t, end : end + HALO, :] = below_ref[f, :, lanes] * scale
-        for i, received in enumerate((left_ref, right_ref)):
-            lanes = slice(i * (width - LANES), i * (width - LANES) + LANES)
-            outer = outer_columns(i, received[f])
-            rim_ref[f, i, first:end, :] = mix(i, velocity[:, lanes], outer) * scale
-            rim_ref[f, i, HALO:first, :] = above_ref[f, :, lanes] * scale
-            rim_ref[f, i, end : end + HALO, :] = below_ref[f, :, lanes] * scale
+        ends = lambda rows: (rows[:, :LANES], rows[:, width - LANES :])
+        outer = outer_columns(left_ref[f], right_ref[f])
+        rim_ref[f, 0, first:end, :] = quarters(*ends(velocity), outer, outer) * scale
+        for received, rows in ((above_ref, slice(HALO, first)), (below_ref, slice(end, end + HALO))):
+            inner = ends(received[f])
+            rim_ref[f, 0, rows, :] = quarters(*inner, *inner) * scale
 
 
 def spread(x, y, *halo):
@@ -441,7 +444,7 @@
         spread_kernel,
         out_shape=[
             jax.ShapeDtypeStruct((2, width // LANES, rows, LANES), jnp.float32),
-            jax.ShapeDtypeStruct((2, 2, rows, LANES), jnp.float32),
+            jax.ShapeDtypeStruct((2, 1, rows, LANES), jnp.float32),
         ],
         in_specs=[vmem] * (2 + len(halo)),
         out_specs=[vmem, vmem],
@@ -471,18 +474,21 @@
     def corner(received, k):
         return received[:, height + k * LANES : height + (k + 1) * LANES]
 
-    for i, (side, received) in enumerate(zip(sides, (from_left, from_right))):
-        field[i, first:end, :] = mix(
-            i, nodal_ref[i * (tiles - 1)], outer_columns(i, received[:, :height])
-        )
-        field[i, HALO:first, :] = mix(i, rows_above[:, side], corner(received, 0))
-        field[i, end : end + HALO, :] = mix(i, rows_below[:, side], corner(received, 1))
-        for f in range(2):
-            speed[f, i, first:end, :] = rim_ref[f, i, first:end, :]
-            for k, rows in enumerate((slice(HALO, first), slice(end, end + HALO))):
-                speed[f, i, rows, :] = mix(
-                    i, rim_ref[f, i, rows, :], corner(received, 2 + 2 * f + k) * (TIME_STEP / 12.0)
-                )
+    ends = lambda rows: (rows[:, sides[0]], rows[:, sides[1]])
+    outer_corner = lambda k: (
+        pltpu.roll(corner(from_right, k), LANES // 2, axis=1), corner(from_left, k)
+    )
+    outer = outer_columns(from_left[:, :height], from_right[:, :height])
+    field[0, first:end, :] = quarters(nodal_ref[0], nodal_ref[tiles - 1], outer, outer)
+    field[0, HALO:first, :] = quarters(*ends(rows_above), *outer_corner(0))
+    field[0, end : end + HALO, :] = quarters(*ends(rows_below), *outer_corner(1))
+    lane = lax.broadcasted_iota(jnp.int32, (HALO, LANES), 1)
+    for f in range(2):
+        speed[f, 0, first:end, :] = rim_ref[f, 0, first:end, :]
+        for k, rows in enumerate((slice(HALO, first), slice(end, end + HALO))):
+            after, before = outer_corner(2 + 2 * f + k)
+            outside = jnp.where(lane < 3 * LANES // 4, after, before) * (TIME_STEP / 12.0)
+            speed[f, 0, rows, :] = jnp.where(lane < LANES // 2, rim_ref[f, 0, rows, :], outside)
     for fetch in fetches:
         fetch.wait()
 
@@ -498,27 +504,31 @@
 
     def store_last(t, place, value):
         lane = lax.broadcasted_iota(jnp.int32, value.shape, 1)
-        wanted = lane < HALO if t == 0 else lane >= LANES - HALO
-        result_ref[t, place, :] = jnp.where(wanted, value, result_ref[t, place, :])
+        result_ref[0, place, :] = jnp.where(lane < HALO, value, result_ref[0, place, :])
+        result_ref[1, place, :] = jnp.where(
+            lane >= LANES - HALO, pltpu.roll(value, LANES // 2, axis=1), result_ref[1, place, :]
+        )
+
+    def after_last(place):
+        for i, side in enumerate(sides):
+            pltpu.make_async_copy(
+                result_ref.at[i, place], out_ref.at[place, pl.ds(side.start, LANES)], sem.at[i]
+            ).start()
 
     heun_loops(
-        field, middle, speed, height, *chunks(height), make_across, store_last, lambda place: None
-    )
-    stores = [
-        pltpu.make_async_copy(result_ref.at[i], out_ref.at[:, pl.ds(side.start, LANES)], sem.at[i])
-        for i, side in enumerate(sides)
-    ]
-    for store in stores:
-        store.start()
-    for store in stores:
-        store.wait()
+        field, middle, speed, height, *chunks(height, 264), make_across, store_last, after_last
+    )
+    for i, side in enumerate(sides):
+        pltpu.make_async_copy(
+            result_ref.at[i], out_ref.at[:, pl.ds(side.start, LANES)], sem.at[i]
+        ).wait()
 
 
 def rim_steps(main, nodal, speed, stencil, *halo):
     _, height, _ = nodal.shape
     vmem = pl.BlockSpec(memory_space=pltpu.VMEM)
     anywhere = pl.BlockSpec(memory_space=pl.ANY)
-    extended = (2, height + 4 * HALO, LANES)
+    extended = (1, height + 4 * HALO, LANES)
     return pl.pallas_call(
         rim_kernel,
         out_shape=jax.ShapeDtypeStruct(main.shape, jnp.float32),
@@ -680,9 +690,10 @@
     share = lead_share(offsets, index_x, index_y, size_x, size_y, tiles_across, tile_height)
     weight = weight_pattern(grid_levels, coefficients, faulty_grids)
     hat = hat_matrix(HAT).astype(jnp.bfloat16)
+    hat_x, hat_y = jnp.concatenate([hat, hat], axis=1), jnp.concatenate([hat.T, hat.T], axis=0)
 
     nodal, first_rows, last_rows, first_cols, last_cols = refine_block(
-        source, slot_rank, incoming, share, weight, hat, hat.T, rows_local, cols_local, tile_height,
+        source, slot_rank, incoming, share, weight, hat_x, hat_y, rows_local, cols_local, tile_height,
         capacity,
     )
     speed_halo, nodal = lax.optimization_barrier((speed_halo, nodal))

time: 105 us -> 104 us (level)
  no operation moved by 1% of the time
where the time goes in v3:
time: 104 us; the launch traced here: 103 us
  waiting for transfers between devices  44 us (42%)
  starting transfers between devices  25.8 us (25%)
  Pallas kernels  23.5 us (23%)
  other arithmetic  7.64 us (7%)
  local copies, waits for them, and re-layouts  1.84 us (2%)
    ppermute x4, waiting for transfers between devices, exchange(): by_inner = lax.ppermute(jnp.where(even, last, first), axis, inner)  41.1 us
    all_to_all x1, starting transfers between devices, local(): lax.all_to_all(outgoing, ('gx', 'gy'), split_axis=0, concat_axis=0, tiled...  11.6 us
    ppermute x4, starting transfers between devices, exchange(): by_outer = lax.ppermute(jnp.where(even, first, last), axis, outer)  11.5 us
    pallas_call x1, Pallas kernels, main_steps(): pl.pallas_call(main_kernel, out_shape=jax.ShapeDtypeStruct((height, tiles...  8.33 us
    pallas_call x1, Pallas kernels, refine_block(): pl.pallas_call(functools.partial(refine_kernel, width // HAT, tile_rows,...  4.78 us
    pallas_call x1, Pallas kernels, rim_steps(): pl.pallas_call(rim_kernel, out_shape=jax.ShapeDtypeStruct(main.shape, jnp...  4.13 us
    select_n x1, other arithmetic, lead_share(): jnp.where(line < row_parts, rows, jnp.where(corner < 0, cols, corners))  3.95 us
    pallas_call x1, Pallas kernels, pack(): pl.pallas_call(functools.partial(pack_kernel, tiles_across, capacity), ou...  3.21 us
  transfers between devices with their start and end apart: 9, of which 4 were waited for; matrix products, arithmetic and copies ran while one was open for 9% of the time, Pallas kernels for 11%

profile of v3, /device:TPU:0, one launch (start us, length us, event | category | flops | bytes accessed | tf_op | source)
XLA Modules:
  0.0 103.3 jit_solution(2529276917540308331)
XLA Ops:
  0.0 3.2 %pack_tiles.1 = f32[128,80,128]{2,1,0:T(8,128)} custom-call(s32[16384]{0:T(1024)} %owner_ref.1, f32[128,16,256]{2,1,0:T(8,128)} %owned_ref.1), custom_call_target="tpu_custom_call" | custom-call | tf_op jit(solution)/shard_map/pack_tiles/pallas_call | solution.py:93
  3.2 11.6 %all-to-all-start = ((f32[128,80,128]{2,1,0:T(8,128)}), f32[128,80,128]{2,1,0:T(8,128)}, u32[]{:S(2)}, u32[]{:S(2)}) async-start(f32[128,80,128]{2,1,0:T(8,128)} %pack_tiles.1), calls=%async_computation | async-start | bytes 10485760 | tf_op jit(solution)/shard_map/all_to_all | solution.py:682
  14.9 0.0 copy-start.2
  14.9 0.0 slice-start
  14.9 0.0 copy-start.4
  14.9 0.0 copy-start.5
  14.9 0.0 copy-start.3
  14.9 2.3 %velocity_edges.1 = (f32[2,8,1024]{2,1,0:T(8,128)}, f32[2,8,1024]{2,1,0:T(8,128)}, f32[2,8,512]{2,1,0:T(8,128)}, f32[2,8,512]{2,1,0:T(8,128)}) custom-call(f32[512,1024]{1,0:T(8,128)} %x_ref.1, f32[512,1024]{1,0:T(8,128)} %x_ref.1, f32[512,1024]{1,0:T(8,128)} %x_ref.1, f32[512,1024]{1,0:T(8,128)} %x_ref.1, f32[512,1024]{1,0:T(8,128)} %y_ref.1, ...), custom_call_target="tpu_custom_call" | custom-call | tf_op jit(solution)/shard_map/velocity_edges/pallas_call | solution.py:569
  17.2 0.9 broadcast_select_fusion.2
  18.1 0.1 collective-permute-start.1
  18.2 2.3 %collective-permute-start = (f32[2,8,1024]{2,1,0:T(8,128)S(1)}, f32[2,8,1024]{2,1,0:T(8,128)S(1)}, u32[]{:S(2)}, u32[]{:S(2)}) collective-permute-start(f32[2,8,1024]{2,1,0:T(8,128)S(1)} %get-tuple-element.50), channel_id=1, source_target_pairs={{16,32},{32,16},{48,64},{64,48},{80,96},{96,80},{112,0},{0,112},{1... | collective-permute-start | bytes 196616 | tf_op jit(solution)/shard_map/ppermute | solution.py:634
  20.4 0.8 broadcast_select_fusion.14
  21.2 1.7 %collective-permute-start.3 = (f32[2,8,512]{2,1,0:T(8,128)S(1)}, f32[2,8,512]{2,1,0:T(8,128)S(1)}, u32[]{:S(2)}, u32[]{:S(2)}) collective-permute-start(f32[2,8,512]{2,1,0:T(8,128)S(1)} %get-tuple-element.67), channel_id=1, source_target_pairs={{0,1},{1,0},{2,3},{3,2},{4,5},{5,4},{6,7},{7,6},{8,9},{9,8},{10,11... | collective-permute-start | bytes 98312 | tf_op jit(solution)/shard_map/ppermute | solution.py:633
  22.9 4.5 %collective-permute-start.2 = (f32[2,8,512]{2,1,0:T(8,128)S(1)}, f32[2,8,512]{2,1,0:T(8,128)S(1)}, u32[]{:S(2)}, u32[]{:S(2)}) collective-permute-start(f32[2,8,512]{2,1,0:T(8,128)S(1)} %get-tuple-element.68), channel_id=1, source_target_pairs={{1,2},{2,1},{3,4},{4,3},{5,6},{6,5},{7,8},{8,7},{9,10},{10,9},{11,... | collective-permute-start | bytes 98312 | tf_op jit(solution)/shard_map/ppermute | solution.py:634
  27.4 0.5 slice.74
  27.9 0.1 slice.73
  28.1 0.1 broadcast_in_dim.118
  28.2 0.1 broadcast_in_dim.119
  28.2 0.1 broadcast_in_dim.120
  28.3 0.7 broadcast_in_dim.121
  29.0 0.1 pad.8.clone
  29.1 0.1 broadcast_in_dim.115
  29.1 0.1 reshape.387
  29.3 0.1 compare_reduce_fusion
  29.5 0.1 select_reduce_fusion.weight_ref
  29.6 0.2 select_convert_fusion
  29.8 0.1 add_add_fusion
  29.9 4.0 %select_select_fusion.2 = (f32[1,128,16,128]{3,2,1,0:T(8,128)S(1)}, f32[1,128,16,128]{3,2,1,0:T(8,128)S(1)}) fusion(s32[16]{0:T(128)S(1)} %get-tuple-element.89, s32[16]{0:T(128)S(1)} %get-tuple-element.90, s32[]{:T(128)S(6)} %axis_index.15, s32[]{:T(128)S(6)} %axis_index.17, s32[16,128]{1,0:T(8,128)S(1)} %add_add_fusion, ...), kind=kLoop, calls=%fused_computation.23 | loop fusion | flops 24641536 | bytes 2105520 | tf_op jit(solution)/shard_map/jit(_where)/select_n | solution.py:657
  33.8 0.1 pad_maximum_fusion.share_ref
  34.0 0.7 fusion.14.stencil_ref
  34.7 0.3 fusion.24
  35.0 0.1 fusion.20.stencil_ref
  35.1 0.2 convert_reduce_fusion.rank_ref
  35.3 41.1 %collective-permute-done.3 = f32[2,8,512]{2,1,0:T(8,128)S(1)} collective-permute-done((f32[2,8,512]{2,1,0:T(8,128)S(1)}, f32[2,8,512]{2,1,0:T(8,128)S(1)}, u32[]{:S(2)}, u32[]{:S(2)}) %collective-permute-start.3) | collective-permute-done | bytes 32800 | tf_op jit(solution)/shard_map/ppermute | solution.py:633
  76.4 1.0 collective-permute-done.2
  77.4 0.0 collective-permute-done.1
  77.4 0.0 collective-permute-done
  77.4 0.5 all-to-all-done.incoming_ref
  77.9 4.8 %refine_block.1 = (f32[8,512,128]{2,1,0:T(8,128)S(1)}, f32[8,1024]{1,0:T(8,128)S(1)}, f32[8,1024]{1,0:T(8,128)S(1)}, f32[8,512]{1,0:T(8,128)S(1)}, f32[8,512]{1,0:T(8,128)S(1)}) custom-call(s32[128]{0:T(128)S(1)} %get-tuple-element.64.source_ref, s32[128]{0:T(128)S(1)} %convert_reduce_fusion.rank_ref, f32[128,80,128]{2,1,0:T(8,128)} %all-to-all-done.incoming_ref, ...), custom_call_target="tpu_custom_call" | custom-call | tf_op jit(solution)/shard_map/refine_block/pallas_call | solution.py:251
  82.7 0.3 collective-permute-start.5
  82.9 2.3 %collective-permute-start.4 = (f32[8,1024]{1,0:T(8,128)S(1)}, f32[8,1024]{1,0:T(8,128)S(1)}, u32[]{:S(2)}, u32[]{:S(2)}) collective-permute-start(f32[8,1024]{1,0:T(8,128)S(1)} %get-tuple-element.62), channel_id=1, source_target_pairs={{16,32},{32,16},{48,64},{64,48},{80,96},{96,80},{112,0},{0,112},{1... | collective-permute-start | bytes 98312 | tf_op jit(solution)/shard_map/ppermute | solution.py:634
  85.3 0.7 spread_velocity.1
  86.1 1.4 %collective-permute-done.4 = f32[8,1024]{1,0:T(8,128)S(1)} collective-permute-done((f32[8,1024]{1,0:T(8,128)S(1)}, f32[8,1024]{1,0:T(8,128)S(1)}, u32[]{:S(2)}, u32[]{:S(2)}) %collective-permute-start.4) | collective-permute-done | bytes 32800 | tf_op jit(solution)/shard_map/ppermute | solution.py:634
  87.6 0.6 collective-permute-start.7
  88.2 2.5 %collective-permute-start.6 = (f32[8,1280]{1,0:T(8,128)S(1)}, f32[8,1280]{1,0:T(8,128)S(1)}, u32[]{:S(2)}, u32[]{:S(2)}) collective-permute-start(f32[8,1280]{1,0:T(8,128)S(1)} %get-tuple-element.54), channel_id=1, source_target_pairs={{1,2},{2,1},{3,4},{4,3},{5,6},{6,5},{7,8},{8,7},{9,10},{10,9},{11,... | collective-permute-start | bytes 122888 | tf_op jit(solution)/shard_map/ppermute | solution.py:634
  90.7 8.3 %heun_main.1.main_ref = f32[512,1024]{1,0:T(8,128)} custom-call(f32[8,512,128]{2,1,0:T(8,128)S(1)} %get-tuple-element.36.nodal_ref, f32[2,8,544,128]{3,2,1,0:T(8,128)S(1)} %get-tuple-element.41.speed, bf16[512,256]{1,0:T(8,128)(2,1)S(1)} %fusion.14.stencil_ref, f32[8,1024]{1,0:T(8,128)S(1)} %get-tuple-element.60.rows_above, ...), custom_call_target="tpu_custom_call" | custom-call | flops 4294967296 | bytes 8388608 | tf_op jit(solution)/shard_map/heun_main/pallas_call | solution.py:387
  99.0 0.0 collective-permute-done.7
  99.0 4.1 %heun_rim.1 = f32[512,1024]{1,0:T(8,128)} custom-call(f32[512,1024]{1,0:T(8,128)} %heun_main.1.main_ref, f32[8,512,128]{2,1,0:T(8,128)S(1)} %get-tuple-element.36.nodal_ref, f32[2,1,544,128]{3,2,1,0:T(8,128)S(1)} %get-tuple-element.44.rim_ref, bf16[256,256]{1,0:T(8,128)(2,1)S(1)} %fusion.20.stencil_ref, ...), custom_call_target="tpu_custom_call", output_to_operand_aliasing={{}: (0, {})} | custom-call | tf_op jit(solution)/shard_map/heun_rim/pallas_call | solution.py:532
  (43 shorter events, 0.2 us)
Async XLA Ops:
  3.2 74.6 %all-to-all-start = ((f32[128,80,128]{2,1,0:T(8,128)}), f32[128,80,128]{2,1,0:T(8,128)}, u32[]{:S(2)}, u32[]{:S(2)}) async-start(f32[128,80,128]{2,1,0:T(8,128)} %pack_tiles.1), calls=%async_computation | async-start | bytes 10485760 | tf_op jit(solution)/shard_map/all_to_all | solution.py:682
  14.9 12.6 %copy-start.2 = (s32[16384]{0:T(1024)S(1)}, s32[16384]{0:T(1024)}, u32[]{:S(2)}) copy-start(s32[16384]{0:T(1024)} %owner_ref.1) | copy-start | bytes 196612
  14.9 14.2 %slice-start = ((s32[16384]{0:T(1024)}), s32[4]{0:T(128)S(1)}, s32[]{:S(2)}) async-start(s32[16384]{0:T(1024)} %owner_ref.1), calls=%async_computation.1 | async-start | bytes 1024 | tf_op jit(solution)/shard_map/slice | solution.py:641
  14.9 14.5 %copy-start.4 = (s32[2]{0:T(128)S(1)}, s32[2]{0:T(128)}, u32[]{:S(2)}) copy-start(s32[2]{0:T(128)} %param.11) | copy-start | bytes 28
  14.9 14.5 %copy-start.5 = (s32[8]{0:T(128)S(1)}, s32[8]{0:T(128)}, u32[]{:S(2)}) copy-start(s32[8]{0:T(128)} %param.10) | copy-start | bytes 100
  14.9 14.5 %copy-start.3 = (s32[8,2]{0,1:T(2,128)S(1)}, s32[8,2]{0,1:T(2,128)}, u32[]{:S(2)}) copy-start(s32[8,2]{0,1:T(2,128)} %param.9) | copy-start | bytes 196
  18.1 59.3 %collective-permute-start.1 = (f32[2,8,1024]{2,1,0:T(8,128)S(1)}, f32[2,8,1024]{2,1,0:T(8,128)S(1)}, u32[]{:S(2)}, u32[]{:S(2)}) collective-permute-start(f32[2,8,1024]{2,1,0:T(8,128)S(1)} %get-tuple-element.49), channel_id=1, source_target_pairs={{0,16},{16,0},{32,48},{48,32},{64,80},{80,64},{96,112},{112,96},{1... | collective-permute-start | bytes 196616 | tf_op jit(solution)/shard_map/ppermute | solution.py:633
  18.2 59.2 %collective-permute-start = (f32[2,8,1024]{2,1,0:T(8,128)S(1)}, f32[2,8,1024]{2,1,0:T(8,128)S(1)}, u32[]{:S(2)}, u32[]{:S(2)}) collective-permute-start(f32[2,8,1024]{2,1,0:T(8,128)S(1)} %get-tuple-element.50), channel_id=1, source_target_pairs={{16,32},{32,16},{48,64},{64,48},{80,96},{96,80},{112,0},{0,112},{1... | collective-permute-start | bytes 196616 | tf_op jit(solution)/shard_map/ppermute | solution.py:634
  21.2 55.2 %collective-permute-start.3 = (f32[2,8,512]{2,1,0:T(8,128)S(1)}, f32[2,8,512]{2,1,0:T(8,128)S(1)}, u32[]{:S(2)}, u32[]{:S(2)}) collective-permute-start(f32[2,8,512]{2,1,0:T(8,128)S(1)} %get-tuple-element.67), channel_id=1, source_target_pairs={{0,1},{1,0},{2,3},{3,2},{4,5},{5,4},{6,7},{7,6},{8,9},{9,8},{10,11... | collective-permute-start | bytes 98312 | tf_op jit(solution)/shard_map/ppermute | solution.py:633
  22.9 54.4 %collective-permute-start.2 = (f32[2,8,512]{2,1,0:T(8,128)S(1)}, f32[2,8,512]{2,1,0:T(8,128)S(1)}, u32[]{:S(2)}, u32[]{:S(2)}) collective-permute-start(f32[2,8,512]{2,1,0:T(8,128)S(1)} %get-tuple-element.68), channel_id=1, source_target_pairs={{1,2},{2,1},{3,4},{4,3},{5,6},{6,5},{7,8},{8,7},{9,10},{10,9},{11,... | collective-permute-start | bytes 98312 | tf_op jit(solution)/shard_map/ppermute | solution.py:634
  77.9 7.4 %copy-start = (f32[512,1024]{1,0:T(8,128)S(1)}, f32[512,1024]{1,0:T(8,128)}, u32[]{:S(2)}) copy-start(f32[512,1024]{1,0:T(8,128)} %x_ref.1) | copy-start | bytes 6291460
  77.9 7.4 %copy-start.1 = (f32[512,1024]{1,0:T(8,128)S(1)}, f32[512,1024]{1,0:T(8,128)}, u32[]{:S(2)}) copy-start(f32[512,1024]{1,0:T(8,128)} %y_ref.1) | copy-start | bytes 6291460
  82.7 3.4 %collective-permute-start.5 = (f32[8,1024]{1,0:T(8,128)S(1)}, f32[8,1024]{1,0:T(8,128)S(1)}, u32[]{:S(2)}, u32[]{:S(2)}) collective-permute-start(f32[8,1024]{1,0:T(8,128)S(1)} %get-tuple-element.61), channel_id=1, source_target_pairs={{0,16},{16,0},{32,48},{48,32},{64,80},{80,64},{96,112},{112,96},{1... | collective-permute-start | bytes 98312 | tf_op jit(solution)/shard_map/ppermute | solution.py:633
  82.9 4.6 %collective-permute-start.4 = (f32[8,1024]{1,0:T(8,128)S(1)}, f32[8,1024]{1,0:T(8,128)S(1)}, u32[]{:S(2)}, u32[]{:S(2)}) collective-permute-start(f32[8,1024]{1,0:T(8,128)S(1)} %get-tuple-element.62), channel_id=1, source_target_pairs={{16,32},{32,16},{48,64},{64,48},{80,96},{96,80},{112,0},{0,112},{1... | collective-permute-start | bytes 98312 | tf_op jit(solution)/shard_map/ppermute | solution.py:634
  87.6 11.4 %collective-permute-start.7 = (f32[8,1280]{1,0:T(8,128)S(1)}, f32[8,1280]{1,0:T(8,128)S(1)}, u32[]{:S(2)}, u32[]{:S(2)}) collective-permute-start(f32[8,1280]{1,0:T(8,128)S(1)} %get-tuple-element.53), channel_id=1, source_target_pairs={{0,1},{1,0},{2,3},{3,2},{4,5},{5,4},{6,7},{7,6},{8,9},{9,8},{10,11... | collective-permute-start | bytes 122888 | tf_op jit(solution)/shard_map/ppermute | solution.py:633
  88.2 10.8 %collective-permute-start.6 = (f32[8,1280]{1,0:T(8,128)S(1)}, f32[8,1280]{1,0:T(8,128)S(1)}, u32[]{:S(2)}, u32[]{:S(2)}) collective-permute-start(f32[8,1280]{1,0:T(8,128)S(1)} %get-tuple-element.54), channel_id=1, source_target_pairs={{1,2},{2,1},{3,4},{4,3},{5,6},{6,5},{7,8},{8,7},{9,10},{10,9},{11,... | collective-permute-start | bytes 122888 | tf_op jit(solution)/shard_map/ppermute | solution.py:634
